TPU v7x, 32 devices: a whole 2x2x4 slice. The times are simulated.
32 devices in a mesh: gx: 4 (over y, x), gy: 4 (over z), gz: 2 (over core).
Axes of the slice: x: 2, y: 2, z: 4, core: 2. Of those that a mesh axis runs over, the one named last changes fastest.
Arguments:
- viscosity: float32 [32, 64, 512], P('gz', 'gy', 'gx'), may hold values from 0.1 to 10
- adjoint_source: float32 [32, 64, 512], P('gz', 'gy', 'gx'), may hold values from -6 to 6
- forward_velocity: float32 [32, 64, 512], P('gz', 'gy', 'gx'), may hold values from -6 to 6
- friction: float32 [64, 512], P('gy', 'gx'), may hold values from 0.1 to 10
- ice_mask: int32 [64, 512], P('gy', 'gx'), may hold values 0 or 1
- grounded_mask: int32 [64, 512], P('gy', 'gx'), may hold values 0 or 1
Outputs:
- adjoint: float32 [32, 64, 512], P('gz', 'gy', 'gx')
- gradient: float32 [64, 512], P('gy', ('gx', 'gz'))
All inputs are finite; a program needn't handle non-finite values. No bound on the sum of `ice_mask` or of `grounded_mask` on one device may be relied on, other than what follows from the above.
Results may differ from a plain program's by a relative error of at most 0.00002.
Values sent between devices are 32-bit elements; how exact they have to be, the bound alone decides.
No kernel may reach another device: no remote copies, remote signals or barrier semaphores. Data moves between devices by JAX's collectives and lax.ppermute only.
A program may use at most 64 MiB of HBM per device.

v0:
```python
import jax
import jax.numpy as jnp
from jax import lax
from jax.sharding import PartitionSpec as P

S0 = 4
S1 = 4
S2 = 8


OMEGA = 0.8
VERT = 4.0
HI = lax.Precision.HIGHEST
FINE_HALO = 12
MID_HALO = 6
POST_HALO = 4
COL_HALO = 64


def layer_halos(u):
    count = lax.axis_size("gz")
    head = u[:1]
    tail = u[-1:]
    if count == 2:
        first = lax.axis_index("gz") == 0
        got = lax.ppermute(jnp.where(first, tail, head), "gz", [(0, 1), (1, 0)])
        zero = jnp.zeros_like(got)
        return jnp.where(first, zero, got), jnp.where(first, got, zero)
    lo = lax.ppermute(tail, "gz", [(i, i + 1) for i in range(count - 1)])
    hi = lax.ppermute(head, "gz", [(i + 1, i) for i in range(count - 1)])
    return lo, hi


def extend_rows(a, h):
    count = lax.axis_size("gy")
    lo = lax.ppermute(a[:, -h:], "gy", [(i, i + 1) for i in range(count - 1)])
    hi = lax.ppermute(a[:, :h], "gy", [(i + 1, i) for i in range(count - 1)])
    return jnp.concatenate([lo, a, hi], axis=1)


def gather_blocks(a, axis):
    count = lax.axis_size(axis)
    got = [a]
    for s in range(1, count):
        got.append(lax.ppermute(a, axis, [(i, (i + s) % count) for i in range(count)]))
    rev = jnp.stack(got[::-1], axis=0)
    return jnp.roll(rev, lax.axis_index(axis) + 1, axis=0)


def extend_cols(a, h):
    count = lax.axis_size("gx")
    lo = lax.ppermute(a[:, :, -h:], "gx", [(i, i + 1) for i in range(count - 1)])
    hi = lax.ppermute(a[:, :, :h], "gx", [(i + 1, i) for i in range(count - 1)])
    return jnp.concatenate([lo, a, hi], axis=2)


def col_mask(own_cols, h):
    g = lax.axis_index("gx") * own_cols - h + lax.broadcasted_iota(jnp.int32, (1, 1, own_cols + 2 * h), 2)
    return (g >= 0) & (g < own_cols * lax.axis_size("gx"))


def crop(a, h_from, h_to):
    cut = h_from - h_to
    return a[:, cut : a.shape[1] - cut]


def row_mask(own_rows, h):
    g = lax.axis_index("gy") * own_rows - h + lax.broadcasted_iota(jnp.int32, (1, own_rows + 2 * h, 1), 1)
    return (g >= 0) & (g < own_rows * lax.axis_size("gy"))


def neighbours(u):
    zlo, zhi = layer_halos(u)
    zero_row = jnp.zeros_like(u[:, :1])
    zero_col = jnp.zeros_like(u[:, :, :1])
    zm = jnp.concatenate([zlo, u[:-1]], axis=0)
    zp = jnp.concatenate([u[1:], zhi], axis=0)
    ym = jnp.concatenate([zero_row, u[:, :-1]], axis=1)
    yp = jnp.concatenate([u[:, 1:], zero_row], axis=1)
    xm = jnp.concatenate([zero_col, u[:, :, :-1]], axis=2)
    xp = jnp.concatenate([u[:, :, 1:], zero_col], axis=2)
    return zm, zp, ym, yp, xm, xp


def face_set(eta):
    zm, zp, ym, yp, xm, xp = neighbours(eta)
    zlo = VERT * (0.5 * (eta + zm))
    zhi = VERT * (0.5 * (eta + zp))
    ylo = 0.5 * (eta + ym)
    yhi = 0.5 * (eta + yp)
    xlo = 0.5 * (eta + xm)
    xhi = 0.5 * (eta + xp)
    return (zlo, zhi, ylo, yhi, xlo, xhi)


def operate(u, coef):
    zlo, zhi, ylo, yhi, xlo, xhi, extra = coef
    zm, zp, ym, yp, xm, xp = neighbours(u)
    out = zlo * (u - zm) + zhi * (u - zp)
    out = out + ylo * (u - ym) + yhi * (u - yp)
    out = out + xlo * (u - xm) + xhi * (u - xp)
    return out + extra * u


def diagonal(coef):
    zlo, zhi, ylo, yhi, xlo, xhi, extra = coef
    return zlo + zhi + ylo + yhi + xlo + xhi + extra


def pick(n, parity):
    src = lax.broadcasted_iota(jnp.int32, (n, n // 2), 0)
    dst = lax.broadcasted_iota(jnp.int32, (n, n // 2), 1)
    return (src == 2 * dst + parity).astype(jnp.float32)


def cols(a, parity):
    return jnp.dot(a, pick(a.shape[-1], parity), precision=HI)


def rows(a, parity):
    return jnp.einsum("yr,zyx->zrx", pick(a.shape[1], parity), a, precision=HI)


def mean_four(a):
    r0 = rows(a, 0)
    r1 = rows(a, 1)
    return 0.25 * (cols(r0, 0) + cols(r1, 0) + cols(r0, 1) + cols(r1, 1))


def coarsen(coef):
    zlo, zhi, ylo, yhi, xlo, xhi, extra = coef
    cxlo = 0.125 * cols(rows(xlo, 0) + rows(xlo, 1), 0)
    cxhi = 0.125 * cols(rows(xhi, 0) + rows(xhi, 1), 1)
    ylo0 = rows(ylo, 0)
    yhi1 = rows(yhi, 1)
    cylo = 0.125 * (cols(ylo0, 0) + cols(ylo0, 1))
    cyhi = 0.125 * (cols(yhi1, 0) + cols(yhi1, 1))
    return (mean_four(zlo), mean_four(zhi), cylo, cyhi, cxlo, cxhi, mean_four(extra))


def coarsen_stacked(coef):
    layers = coef[0].shape[0]
    width = coef[0].shape[2]
    half = width // 2
    stack = jnp.concatenate(coef, axis=0)
    both_rows = jnp.concatenate([rows(stack, 0), rows(stack, 1)], axis=0)
    src = lax.broadcasted_iota(jnp.int32, (width, width), 0)
    dst = lax.broadcasted_iota(jnp.int32, (width, width), 1)
    want = jnp.where(dst < half, 2 * dst, 2 * (dst - half) + 1)
    picked = jnp.dot(both_rows, (src == want).astype(jnp.float32), precision=HI)
    count = len(coef)

    def part(k, odd_row, odd_col):
        at = (odd_row * count + k) * layers
        return picked[at : at + layers, :, odd_col * half : (odd_col + 1) * half]

    def four(k):
        return 0.25 * (part(k, 0, 0) + part(k, 1, 0) + part(k, 0, 1) + part(k, 1, 1))

    cxlo = 0.125 * (part(4, 0, 0) + part(4, 1, 0))
    cxhi = 0.125 * (part(5, 0, 1) + part(5, 1, 1))
    cylo = 0.125 * (part(2, 0, 0) + part(2, 0, 1))
    cyhi = 0.125 * (part(3, 1, 0) + part(3, 1, 1))
    return (four(0), four(1), cylo, cyhi, cxlo, cxhi, four(6))


def spread(n):
    src = lax.broadcasted_iota(jnp.int32, (n, 2 * n), 0)
    dst = lax.broadcasted_iota(jnp.int32, (n, 2 * n), 1)
    return (src == dst // 2).astype(jnp.float32)


def prolong(field):
    wide = jnp.dot(field, spread(field.shape[-1]), precision=HI)
    return jnp.einsum("ry,zrx->zyx", spread(field.shape[1]), wide, precision=HI)


def sweep(field, rhs, coef, diag, inside):
    new = field + OMEGA * (rhs - operate(field, coef)) / diag
    return jnp.where(inside, new, 0.0)


def smooth(field, rhs, coef, diag, inside, count):
    for i in range(count):
        field = sweep(field, rhs, coef, diag, inside)
    return field


def crop_all(arrs, h_from, h_to):
    return tuple(crop(a, h_from, h_to) for a in arrs)


def body_wide(viscosity, adjoint_source, forward_velocity, friction, ice_mask, grounded_mask):
    layers = viscosity.shape[0]
    own_rows = viscosity.shape[1]
    mid_rows = own_rows // 2
    cols_own = viscosity.shape[2]
    half_cols = cols_own // 2
    gz = lax.axis_index("gz")
    gy = lax.axis_index("gy")
    total_layers = layers * lax.axis_size("gz")
    layer = (gz * layers + jnp.arange(layers)).astype(jnp.float32)
    profile = (jnp.float32(total_layers) - layer) / jnp.float32(total_layers)
    wsq = profile * profile
    icef = ice_mask.astype(jnp.float32)
    groundf = grounded_mask.astype(jnp.float32)
    base = 0.05 + 2.0 * (1.0 - icef)
    ground_fric = groundf * friction
    stacked = jnp.concatenate([viscosity, adjoint_source, base[None], ground_fric[None]], axis=0)
    hv = FINE_HALO + 1
    wide = extend_cols(stacked, COL_HALO)
    ext = extend_rows(jnp.concatenate([wide[:layers], wide[2 * layers :]], axis=0), hv)
    src_e = crop(extend_rows(wide[layers : 2 * layers], hv), hv, FINE_HALO)
    visc_e = ext[:layers]
    base_e = crop(ext[layers : layers + 1], hv, FINE_HALO)[0]
    gfr_e = crop(ext[layers + 1 : layers + 2], hv, FINE_HALO)[0]
    extra = base_e[None, :, :] + gfr_e[None, :, :] * wsq[:, None, None]
    fine = crop_all(face_set(visc_e), hv, FINE_HALO) + (extra,)
    dfine = diagonal(fine)
    middle = coarsen_stacked(fine)
    dmid = diagonal(middle)
    coarse_own = coarsen_stacked(crop_all(middle, FINE_HALO // 2, 0))
    coarse_all = gather_blocks(jnp.concatenate(coarse_own, axis=0), "gy")
    coarse_all = jnp.concatenate([coarse_all[i] for i in range(coarse_all.shape[0])], axis=1)
    coarse = tuple(coarse_all[i * layers : (i + 1) * layers] for i in range(7))
    dcoarse = diagonal(coarse)
    in_fine = row_mask(own_rows, FINE_HALO) & col_mask(cols_own, COL_HALO)
    in_mid = row_mask(mid_rows, FINE_HALO // 2) & col_mask(cols_own // 2, COL_HALO // 2)

    lam = jnp.where(in_fine, OMEGA * src_e / dfine, 0.0)
    lam = smooth(lam, src_e, fine, dfine, in_fine, S0 - 1)
    b_mid = mean_four(src_e - operate(lam, fine))
    e_mid = jnp.where(in_mid, OMEGA * b_mid / dmid, 0.0)
    e_mid = smooth(e_mid, b_mid, middle, dmid, in_mid, S1 - 1)
    hm = FINE_HALO // 2
    res_mid = crop(b_mid - operate(e_mid, middle), hm, 0)
    b_low = gather_blocks(mean_four(res_mid), "gy")
    b_low = jnp.concatenate([b_low[i] for i in range(b_low.shape[0])], axis=1)
    ones = col_mask(cols_own // 4, COL_HALO // 4)
    e_low = jnp.where(ones, OMEGA * b_low / dcoarse, 0.0)
    e_low = smooth(e_low, b_low, coarse, dcoarse, ones, S2 - 1)

    pair = jnp.concatenate([crop(e_mid, hm, 0), crop(b_mid, hm, 0)], axis=0)
    pair = extend_rows(pair, MID_HALO)
    e_mid = pair[:layers]
    b_mid = pair[layers:]
    low_rows = own_rows // 4
    ch = MID_HALO // 2
    padded = jnp.pad(e_low, ((0, 0), (ch, ch), (0, 0)))
    e_near = lax.dynamic_slice_in_dim(padded, gy * low_rows, low_rows + 2 * ch, 1)
    e_mid = e_mid + prolong(e_near)
    middle_p = crop_all(middle, hm, MID_HALO)
    dmid_p = crop(dmid, hm, MID_HALO)
    in_mid_p = row_mask(mid_rows, MID_HALO) & col_mask(cols_own // 2, COL_HALO // 2)
    e_mid = smooth(e_mid, b_mid, middle_p, dmid_p, in_mid_p, S1)

    lam = crop(lam, FINE_HALO, POST_HALO) + prolong(crop(e_mid, MID_HALO, POST_HALO // 2))
    fine_p = crop_all(fine, FINE_HALO, POST_HALO)
    dfine_p = crop(dfine, FINE_HALO, POST_HALO)
    src_p = crop(src_e, FINE_HALO, POST_HALO)
    in_fine_p = row_mask(own_rows, POST_HALO) & col_mask(cols_own, COL_HALO)
    lam = smooth(lam, src_p, fine_p, dfine_p, in_fine_p, S0)
    lam = crop(lam, POST_HALO, 0)

    own = lam[:, :, COL_HALO : COL_HALO + cols_own]
    column = jnp.sum(wsq[:, None, None] * forward_velocity * own, axis=0)
    parts = gather_blocks(column, "gz")
    summed = parts[0]
    for k in range(1, parts.shape[0]):
        summed = summed + parts[k]
    terms = -ground_fric * summed
    gradient = lax.dynamic_slice_in_dim(terms, gz * half_cols, half_cols, 1)
    return (own, gradient)


def n_layer_halos(u):
    count = lax.axis_size("gz")
    head = u[:1]
    tail = u[-1:]
    if count == 2:
        first = lax.axis_index("gz") == 0
        got = lax.ppermute(jnp.where(first, tail, head), "gz", [(0, 1), (1, 0)])
        zero = jnp.zeros_like(got)
        return jnp.where(first, zero, got), jnp.where(first, got, zero)
    lo = lax.ppermute(tail, "gz", [(i, i + 1) for i in range(count - 1)])
    hi = lax.ppermute(head, "gz", [(i + 1, i) for i in range(count - 1)])
    return lo, hi


def n_row_halos(u):
    count = lax.axis_size("gy")
    lo = lax.ppermute(u[:, -1:], "gy", [(i, i + 1) for i in range(count - 1)])
    hi = lax.ppermute(u[:, :1], "gy", [(i + 1, i) for i in range(count - 1)])
    return lo, hi


def n_neighbours(u):
    zlo, zhi = n_layer_halos(u)
    ylo, yhi = n_row_halos(u)
    zero = jnp.zeros_like(u[:, :, :1])
    zm = jnp.concatenate([zlo, u[:-1]], axis=0)
    zp = jnp.concatenate([u[1:], zhi], axis=0)
    ym = jnp.concatenate([ylo, u[:, :-1]], axis=1)
    yp = jnp.concatenate([u[:, 1:], yhi], axis=1)
    xm = jnp.concatenate([zero, u[:, :, :-1]], axis=2)
    xp = jnp.concatenate([u[:, :, 1:], zero], axis=2)
    return zm, zp, ym, yp, xm, xp


def n_face_set(eta):
    zm, zp, ym, yp, xm, xp = n_neighbours(eta)
    zlo = VERT * (0.5 * (eta + zm))
    zhi = VERT * (0.5 * (eta + zp))
    ylo = 0.5 * (eta + ym)
    yhi = 0.5 * (eta + yp)
    xlo = 0.5 * (eta + xm)
    xhi = 0.5 * (eta + xp)
    return (zlo, zhi, ylo, yhi, xlo, xhi)


def n_operate(u, coef):
    zlo, zhi, ylo, yhi, xlo, xhi, extra = coef
    zm, zp, ym, yp, xm, xp = n_neighbours(u)
    out = zlo * (u - zm) + zhi * (u - zp)
    out = out + ylo * (u - ym) + yhi * (u - yp)
    out = out + xlo * (u - xm) + xhi * (u - xp)
    return out + extra * u


def n_diagonal(coef):
    zlo, zhi, ylo, yhi, xlo, xhi, extra = coef
    return zlo + zhi + ylo + yhi + xlo + xhi + extra


def n_pick_matrix(cols):
    half = cols // 2
    src = lax.broadcasted_iota(jnp.int32, (cols, cols), 0)
    dst = lax.broadcasted_iota(jnp.int32, (cols, cols), 1)
    want = jnp.where(dst < half, 2 * dst, 2 * (dst - half) + 1)
    return (src == want).astype(jnp.float32)


def n_split_x(a):
    cols = a.shape[-1]
    both = jnp.dot(a, n_pick_matrix(cols), precision=HI)
    return both[..., : cols // 2], both[..., cols // 2 :]


def n_mean_four(a):
    e0, o0 = n_split_x(a[:, 0::2])
    e1, o1 = n_split_x(a[:, 1::2])
    return 0.25 * (e0 + e1 + o0 + o1)


def n_coarsen(coef):
    zlo, zhi, ylo, yhi, xlo, xhi, extra = coef
    xlo_e, _ = n_split_x(xlo[:, 0::2] + xlo[:, 1::2])
    _, xhi_o = n_split_x(xhi[:, 0::2] + xhi[:, 1::2])
    ylo_e, ylo_o = n_split_x(ylo[:, 0::2])
    yhi_e, yhi_o = n_split_x(yhi[:, 1::2])
    cxlo = 0.125 * xlo_e
    cxhi = 0.125 * xhi_o
    cylo = 0.125 * (ylo_e + ylo_o)
    cyhi = 0.125 * (yhi_e + yhi_o)
    return (n_mean_four(zlo), n_mean_four(zhi), cylo, cyhi, cxlo, cxhi, n_mean_four(extra))


def n_prolong(field):
    cols = field.shape[-1]
    src = lax.broadcasted_iota(jnp.int32, (cols, 2 * cols), 0)
    dst = lax.broadcasted_iota(jnp.int32, (cols, 2 * cols), 1)
    spread = (src == dst // 2).astype(jnp.float32)
    wide = jnp.dot(field, spread, precision=HI)
    return jnp.repeat(wide, 2, axis=1)


def n_sweep(field, rhs, coef, diag):
    return field + OMEGA * (rhs - n_operate(field, coef)) / diag


def n_body(viscosity, adjoint_source, forward_velocity, friction, ice_mask, grounded_mask):
    layers = viscosity.shape[0]
    cols = viscosity.shape[2]
    half_cols = cols // 2
    gz = lax.axis_index("gz")
    total_layers = layers * lax.axis_size("gz")
    layer = (gz * layers + jnp.arange(layers)).astype(jnp.float32)
    profile = (jnp.float32(total_layers) - layer) / jnp.float32(total_layers)
    wsq = profile * profile
    icef = ice_mask.astype(jnp.float32)
    groundf = grounded_mask.astype(jnp.float32)
    base = 0.05 + 2.0 * (1.0 - icef)
    ground_fric = groundf * friction
    stacked = jnp.concatenate([viscosity, adjoint_source, base[None], ground_fric[None]], axis=0)
    gathered = lax.all_gather(stacked, "gx", axis=0, tiled=False)
    count_x = gathered.shape[0]
    gathered = jnp.concatenate([gathered[i] for i in range(count_x)], axis=2)
    visc_all = gathered[:layers]
    source_all = gathered[layers : 2 * layers]
    base_all = gathered[2 * layers]
    gfr_all = gathered[2 * layers + 1]
    extra = base_all[None, :, :] + gfr_all[None, :, :] * wsq[:, None, None]
    fine = n_face_set(visc_all) + (extra,)
    dfine = n_diagonal(fine)
    middle = n_coarsen(fine)
    dmid = n_diagonal(middle)
    coarse = n_coarsen(middle)
    dcoarse = n_diagonal(coarse)
    lam = OMEGA * source_all / dfine
    for i in range(S0 - 1):
        lam = n_sweep(lam, source_all, fine, dfine)
    b_mid = n_mean_four(source_all - n_operate(lam, fine))
    e_mid = OMEGA * b_mid / dmid
    for i in range(S1 - 1):
        e_mid = n_sweep(e_mid, b_mid, middle, dmid)
    b_low = n_mean_four(b_mid - n_operate(e_mid, middle))
    e_low = OMEGA * b_low / dcoarse
    for i in range(S2 - 1):
        e_low = n_sweep(e_low, b_low, coarse, dcoarse)
    e_mid = e_mid + n_prolong(e_low)
    for i in range(S1):
        e_mid = n_sweep(e_mid, b_mid, middle, dmid)
    lam = lam + n_prolong(e_mid)
    for i in range(S0):
        lam = n_sweep(lam, source_all, fine, dfine)
    own = lax.dynamic_slice_in_dim(lam, lax.axis_index("gx") * cols, cols, 2)
    column = jnp.sum(wsq[:, None, None] * forward_velocity * own, axis=0)
    summed = lax.psum(column, "gz")
    terms = -ground_fric * summed
    gradient = lax.dynamic_slice_in_dim(terms, gz * half_cols, half_cols, 1)
    return (own, gradient)


def body(viscosity, *rest):
    layers, own_rows, cols_own = viscosity.shape
    cols_all = cols_own + 2 * COL_HALO
    wide_bytes = 4 * layers * (own_rows + 2 * FINE_HALO + 2) * cols_all
    if COL_HALO <= cols_own and FINE_HALO + 1 <= own_rows and MID_HALO <= own_rows // 2 and 20 * wide_bytes <= 40 * 2**20 and lax.axis_size("gy") <= 8:
        return body_wide(viscosity, *rest)
    return n_body(viscosity, *rest)


def solution(mesh):
    placed = (
        P("gz", "gy", "gx"),
        P("gz", "gy", "gx"),
        P("gz", "gy", "gx"),
        P("gy", "gx"),
        P("gy", "gx"),
        P("gy", "gx"),
    )
    return jax.shard_map(
        body,
        mesh=mesh,
        in_specs=placed,
        out_specs=(P("gz", "gy", "gx"), P("gy", ("gx", "gz"))),
        check_vma=False,
    )
```

profile of v0, /device:TPU:0, one launch (start us, length us, event | category | flops | bytes accessed | tf_op | source)
XLA Modules:
  0.0 139.4 jit_solution(15685641565764314617)
XLA Ops:
  3.2 4.9 %collective-permute-start = (f32[34,16,64]{2,1,0:T(8,128)S(1)}, f32[34,16,64]{2,1,0:T(8,128)S(1)}, u32[]{:S(2)}, u32[]{:S(2)}) collective-permute-start(f32[34,16,64]{2,1,0:T(8,128)S(1)} %get-tuple-element.112), channel_id=1, source_target_pairs={{0,8},{8,16},{16,24},{1,9},{9,17},{17,25},{2,10},{10,18},{18,26},{... | collective-permute-start | bytes 417800 | tf_op jit(solution)/shard_map/ppermute | solution.py:52
  8.1 1.3 collective-permute-start.1
  10.1 3.9 %collective-permute-done = f32[34,16,64]{2,1,0:T(8,128)S(1)} collective-permute-done((f32[34,16,64]{2,1,0:T(8,128)S(1)}, f32[34,16,64]{2,1,0:T(8,128)S(1)}, u32[]{:S(2)}, u32[]{:S(2)}) %collective-permute-start) | collective-permute-done | bytes 139296 | tf_op jit(solution)/shard_map/ppermute | solution.py:52
  14.0 7.9 %collective-permute-done.1 = f32[34,16,64]{2,1,0:T(8,128)S(1)} collective-permute-done((f32[34,16,64]{2,1,0:T(8,128)S(1)}, f32[34,16,64]{2,1,0:T(8,128)S(1)}, u32[]{:S(2)}, u32[]{:S(2)}) %collective-permute-start.1) | collective-permute-done | bytes 139296 | tf_op jit(solution)/shard_map/ppermute | solution.py:53
  23.3 3.5 %collective-permute-start.2 = (f32[16,13,256]{2,1,0:T(8,128)S(1)}, f32[16,13,256]{2,1,0:T(8,128)S(1)}, u32[]{:S(2)}, u32[]{:S(2)}) collective-permute-start(f32[16,13,256]{2,1,0:T(8,128)S(1)} %get-tuple-element.82), channel_id=1, source_target_pairs={{0,2},{2,4},{4,6},{1,3},{3,5},{5,7},{8,10},{10,12},{12,14},{9,11},... | collective-permute-start | bytes 638984 | tf_op jit(solution)/shard_map/ppermute | solution.py:36
  26.8 1.3 collective-permute-start.3
  28.2 4.6 %collective-permute-start.4 = (f32[18,13,256]{2,1,0:T(8,128)S(1)}, f32[18,13,256]{2,1,0:T(8,128)S(1)}, u32[]{:S(2)}, u32[]{:S(2)}) collective-permute-start(f32[18,13,256]{2,1,0:T(8,128)S(1)} %get-tuple-element.110), channel_id=1, source_target_pairs={{0,2},{2,4},{4,6},{1,3},{3,5},{5,7},{8,10},{10,12},{12,14},{9,11},... | collective-permute-start | bytes 718856 | tf_op jit(solution)/shard_map/ppermute | solution.py:36
  34.1 1.5 %collective-permute-done.3 = f32[16,13,256]{2,1,0:T(8,128)S(1)} collective-permute-done((f32[16,13,256]{2,1,0:T(8,128)S(1)}, f32[16,13,256]{2,1,0:T(8,128)S(1)}, u32[]{:S(2)}, u32[]{:S(2)}) %collective-permute-start.3) | collective-permute-done | bytes 213024 | tf_op jit(solution)/shard_map/ppermute | solution.py:37
  35.8 2.0 %collective-permute-done.4 = f32[18,13,256]{2,1,0:T(8,128)S(1)} collective-permute-done((f32[18,13,256]{2,1,0:T(8,128)S(1)}, f32[18,13,256]{2,1,0:T(8,128)S(1)}, u32[]{:S(2)}, u32[]{:S(2)}) %collective-permute-start.4) | collective-permute-done | bytes 239648 | tf_op jit(solution)/shard_map/ppermute | solution.py:36
  37.7 4.1 %collective-permute-done.5 = f32[18,13,256]{2,1,0:T(8,128)S(1)} collective-permute-done((f32[18,13,256]{2,1,0:T(8,128)S(1)}, f32[18,13,256]{2,1,0:T(8,128)S(1)}, u32[]{:S(2)}, u32[]{:S(2)}) %collective-permute-start.5) | collective-permute-done | bytes 239648 | tf_op jit(solution)/shard_map/ppermute | solution.py:37
  45.8 1.8 %fusion.371 = f32[112,256,20]{1,2,0:T(8,128)S(1)} fusion(f32[112,40,256]{2,1,0:T(8,128)S(1)} %fusion.53, s32[20]{0:T(128)S(1)} %iota_multiply_fusion.4), kind=kOutput, calls=%fused_computation.606 | convolution fusion | flops 275252000 | bytes 6881360 | tf_op jit(solution)/shard_map/yr,zyx->zrx/dot_general | solution.py:121
  47.6 1.9 %fusion.375 = f32[112,256,20]{1,2,0:T(8,128)S(1)} fusion(f32[112,40,256]{2,1,0:T(8,128)S(1)} %fusion.53, s32[20]{0:T(128)S(1)} %broadcast_add_fusion.7), kind=kOutput, calls=%fused_computation.608 | convolution fusion | flops 275252000 | bytes 6881360 | tf_op jit(solution)/shard_map/yr,zyx->zrx/dot_general | solution.py:121
  49.6 1.4 copy_bitcast_fusion
  50.9 2.2 %fusion = f32[224,20,256]{2,0,1:T(8,128)S(1)} fusion(f32[112,20,256]{2,0,1:T(8,128)S(1)} %get-tuple-element.270, f32[112,20,256]{2,0,1:T(8,128)S(1)} %get-tuple-element.271, s32[256]{0:T(256)S(1)} %get-tuple-element.273, s32[256]{0:T(256)S(1)} %get-tuple-element.272, pred[256]{0:T(512)(128)(4,1)S(1)} %iota_compare_fusion.8), kind=kOutput, calls=%fused_computation | convolution fusion | flops 3524493312 | bytes 9177344 | tf_op jit(solution)/shard_map/dot_general | solution.py:150
  54.0 2.8 %add_add_fusion = (f32[16,20,128]{2,1,0:T(8,128)S(1)}, f32[16,20,128]{2,1,0:T(8,128)S(1)}, f32[16,20,128]{2,1,0:T(8,128)S(1)}, f32[16,20,128]{2,1,0:T(8,128)S(1)...) fusion(f32[16,20,128]{2,0,1:T(8,128)S(1)} %get-tuple-element.29, ...), kind=kLoop, calls=%fused_computation.299 | loop fusion | flops 1064960 | bytes 4587520 | tf_op jit(solution)/shard_map/add | solution.py:107
  78.1 1.6 %collective-permute-start.17 = (f32[16,4,64]{2,0,1:T(8,128)S(1)}, f32[16,4,64]{2,0,1:T(8,128)S(1)}, u32[]{:S(2)}, u32[]{:S(2)}) collective-permute-start(f32[16,4,64]{2,0,1:T(8,128)S(1)} %fusion.5), channel_id=1, source_target_pairs={{0,6},{2,0},{4,2},{6,4},{1,7},{3,1},{5,3},{7,5},{8,14},{10,8},{12,... | collective-permute-start | bytes 49160 | tf_op jit(solution)/shard_map/ppermute | solution.py:45
  79.7 1.5 %collective-permute-start.18 = (f32[16,4,64]{2,0,1:T(8,128)S(1)}, f32[16,4,64]{2,0,1:T(8,128)S(1)}, u32[]{:S(2)}, u32[]{:S(2)}) collective-permute-start(f32[16,4,64]{2,0,1:T(8,128)S(1)} %fusion.5), channel_id=1, source_target_pairs={{0,4},{2,6},{4,0},{6,2},{1,5},{3,7},{5,1},{7,3},{8,12},{10,14},{12... | collective-permute-start | bytes 49160 | tf_op jit(solution)/shard_map/ppermute | solution.py:45
  81.2 1.6 %collective-permute-start.19 = (f32[16,4,64]{2,0,1:T(8,128)S(1)}, f32[16,4,64]{2,0,1:T(8,128)S(1)}, u32[]{:S(2)}, u32[]{:S(2)}) collective-permute-start(f32[16,4,64]{2,0,1:T(8,128)S(1)} %fusion.5), channel_id=1, source_target_pairs={{0,2},{2,4},{4,6},{6,0},{1,3},{3,5},{5,7},{7,1},{8,10},{10,12},{12... | collective-permute-start | bytes 49160 | tf_op jit(solution)/shard_map/ppermute | solution.py:45
  84.5 2.3 %collective-permute-start.20 = (f32[112,4,64]{2,0,1:T(8,128)S(1)}, f32[112,4,64]{2,0,1:T(8,128)S(1)}, u32[]{:S(2)}, u32[]{:S(2)}) collective-permute-start(f32[112,4,64]{2,0,1:T(8,128)S(1)} %constant_dynamic-update-slice_fusion.15), channel_id=1, source_target_pairs={{0,6},{2,0},{4,2},{6,4},{1,7},{3,1},{5,3},{7,5},{8,14},{10,8},{12,... | collective-permute-start | bytes 344072 | tf_op jit(solution)/shard_map/ppermute | solution.py:45
  87.6 4.7 %collective-permute-start.14 = (f32[32,6,128]{2,1,0:T(8,128)S(1)}, f32[32,6,128]{2,1,0:T(8,128)S(1)}, u32[]{:S(2)}, u32[]{:S(2)}) collective-permute-start(f32[32,6,128]{2,1,0:T(8,128)S(1)} %get-tuple-element.217), channel_id=1, source_target_pairs={{0,2},{2,4},{4,6},{1,3},{3,5},{5,7},{8,10},{10,12},{12,14},{9,11},... | collective-permute-start | bytes 294920 | tf_op jit(solution)/shard_map/ppermute | solution.py:36
  92.3 1.3 collective-permute-start.15
  93.7 10.2 %collective-permute-done.14 = f32[32,6,128]{2,1,0:T(8,128)S(1)} collective-permute-done((f32[32,6,128]{2,1,0:T(8,128)S(1)}, f32[32,6,128]{2,1,0:T(8,128)S(1)}, u32[]{:S(2)}, u32[]{:S(2)}) %collective-permute-start.14) | collective-permute-done | bytes 98336 | tf_op jit(solution)/shard_map/ppermute | solution.py:36
  103.9 2.3 %collective-permute-done.15 = f32[32,6,128]{2,1,0:T(8,128)S(1)} collective-permute-done((f32[32,6,128]{2,1,0:T(8,128)S(1)}, f32[32,6,128]{2,1,0:T(8,128)S(1)}, u32[]{:S(2)}, u32[]{:S(2)}) %collective-permute-start.15) | collective-permute-done | bytes 98336 | tf_op jit(solution)/shard_map/ppermute | solution.py:37
  106.3 1.4 %collective-permute-done.21 = f32[112,4,64]{2,0,1:T(8,128)S(1)} collective-permute-done((f32[112,4,64]{2,0,1:T(8,128)S(1)}, f32[112,4,64]{2,0,1:T(8,128)S(1)}, u32[]{:S(2)}, u32[]{:S(2)}) %collective-permute-start.21) | collective-permute-done | bytes 114720 | tf_op jit(solution)/shard_map/ppermute | solution.py:45
  (326 shorter events, 65.1 us)
Async XLA Ops:
  3.2 10.7 %collective-permute-start = (f32[34,16,64]{2,1,0:T(8,128)S(1)}, f32[34,16,64]{2,1,0:T(8,128)S(1)}, u32[]{:S(2)}, u32[]{:S(2)}) collective-permute-start(f32[34,16,64]{2,1,0:T(8,128)S(1)} %get-tuple-element.112), channel_id=1, source_target_pairs={{0,8},{8,16},{16,24},{1,9},{9,17},{17,25},{2,10},{10,18},{18,26},{... | collective-permute-start | bytes 417800 | tf_op jit(solution)/shard_map/ppermute | solution.py:52
  8.1 13.8 %collective-permute-start.1 = (f32[34,16,64]{2,1,0:T(8,128)S(1)}, f32[34,16,64]{2,1,0:T(8,128)S(1)}, u32[]{:S(2)}, u32[]{:S(2)}) collective-permute-start(f32[34,16,64]{2,1,0:T(8,128)S(1)} %get-tuple-element.113), channel_id=1, source_target_pairs={{8,0},{16,8},{24,16},{9,1},{17,9},{25,17},{10,2},{18,10},{26,18},{... | collective-permute-start | bytes 417800 | tf_op jit(solution)/shard_map/ppermute | solution.py:53
  23.3 10.8 %collective-permute-start.2 = (f32[16,13,256]{2,1,0:T(8,128)S(1)}, f32[16,13,256]{2,1,0:T(8,128)S(1)}, u32[]{:S(2)}, u32[]{:S(2)}) collective-permute-start(f32[16,13,256]{2,1,0:T(8,128)S(1)} %get-tuple-element.82), channel_id=1, source_target_pairs={{0,2},{2,4},{4,6},{1,3},{3,5},{5,7},{8,10},{10,12},{12,14},{9,11},... | collective-permute-start | bytes 638984 | tf_op jit(solution)/shard_map/ppermute | solution.py:36
  26.8 8.9 %collective-permute-start.3 = (f32[16,13,256]{2,1,0:T(8,128)S(1)}, f32[16,13,256]{2,1,0:T(8,128)S(1)}, u32[]{:S(2)}, u32[]{:S(2)}) collective-permute-start(f32[16,13,256]{2,1,0:T(8,128)S(1)} %get-tuple-element.83), channel_id=1, source_target_pairs={{2,0},{4,2},{6,4},{3,1},{5,3},{7,5},{10,8},{12,10},{14,12},{11,9},... | collective-permute-start | bytes 638984 | tf_op jit(solution)/shard_map/ppermute | solution.py:37
  28.2 9.5 %collective-permute-start.4 = (f32[18,13,256]{2,1,0:T(8,128)S(1)}, f32[18,13,256]{2,1,0:T(8,128)S(1)}, u32[]{:S(2)}, u32[]{:S(2)}) collective-permute-start(f32[18,13,256]{2,1,0:T(8,128)S(1)} %get-tuple-element.110), channel_id=1, source_target_pairs={{0,2},{2,4},{4,6},{1,3},{3,5},{5,7},{8,10},{10,12},{12,14},{9,11},... | collective-permute-start | bytes 718856 | tf_op jit(solution)/shard_map/ppermute | solution.py:36
  32.8 9.1 %collective-permute-start.5 = (f32[18,13,256]{2,1,0:T(8,128)S(1)}, f32[18,13,256]{2,1,0:T(8,128)S(1)}, u32[]{:S(2)}, u32[]{:S(2)}) collective-permute-start(f32[18,13,256]{2,1,0:T(8,128)S(1)} %get-tuple-element.111), channel_id=1, source_target_pairs={{2,0},{4,2},{6,4},{3,1},{5,3},{7,5},{10,8},{12,10},{14,12},{11,9},... | collective-permute-start | bytes 718856 | tf_op jit(solution)/shard_map/ppermute | solution.py:37
  42.6 1.3 collective-permute-start.6
  56.8 1.3 collective-permute-start.7
  59.6 1.3 collective-permute-start.8
  62.5 1.3 collective-permute-start.9
  65.4 1.3 collective-permute-start.10
  70.1 1.2 collective-permute-start.11
  78.1 8.7 %collective-permute-start.17 = (f32[16,4,64]{2,0,1:T(8,128)S(1)}, f32[16,4,64]{2,0,1:T(8,128)S(1)}, u32[]{:S(2)}, u32[]{:S(2)}) collective-permute-start(f32[16,4,64]{2,0,1:T(8,128)S(1)} %fusion.5), channel_id=1, source_target_pairs={{0,6},{2,0},{4,2},{6,4},{1,7},{3,1},{5,3},{7,5},{8,14},{10,8},{12,... | collective-permute-start | bytes 49160 | tf_op jit(solution)/shard_map/ppermute | solution.py:45
  79.7 7.8 %collective-permute-start.18 = (f32[16,4,64]{2,0,1:T(8,128)S(1)}, f32[16,4,64]{2,0,1:T(8,128)S(1)}, u32[]{:S(2)}, u32[]{:S(2)}) collective-permute-start(f32[16,4,64]{2,0,1:T(8,128)S(1)} %fusion.5), channel_id=1, source_target_pairs={{0,4},{2,6},{4,0},{6,2},{1,5},{3,7},{5,1},{7,3},{8,12},{10,14},{12... | collective-permute-start | bytes 49160 | tf_op jit(solution)/shard_map/ppermute | solution.py:45
  81.2 11.1 %collective-permute-start.19 = (f32[16,4,64]{2,0,1:T(8,128)S(1)}, f32[16,4,64]{2,0,1:T(8,128)S(1)}, u32[]{:S(2)}, u32[]{:S(2)}) collective-permute-start(f32[16,4,64]{2,0,1:T(8,128)S(1)} %fusion.5), channel_id=1, source_target_pairs={{0,2},{2,4},{4,6},{6,0},{1,3},{3,5},{5,7},{7,1},{8,10},{10,12},{12... | collective-permute-start | bytes 49160 | tf_op jit(solution)/shard_map/ppermute | solution.py:45
  84.5 21.8 %collective-permute-start.20 = (f32[112,4,64]{2,0,1:T(8,128)S(1)}, f32[112,4,64]{2,0,1:T(8,128)S(1)}, u32[]{:S(2)}, u32[]{:S(2)}) collective-permute-start(f32[112,4,64]{2,0,1:T(8,128)S(1)} %constant_dynamic-update-slice_fusion.15), channel_id=1, source_target_pairs={{0,6},{2,0},{4,2},{6,4},{1,7},{3,1},{5,3},{7,5},{8,14},{10,8},{12,... | collective-permute-start | bytes 344072 | tf_op jit(solution)/shard_map/ppermute | solution.py:45
  86.8 21.0 %collective-permute-start.21 = (f32[112,4,64]{2,0,1:T(8,128)S(1)}, f32[112,4,64]{2,0,1:T(8,128)S(1)}, u32[]{:S(2)}, u32[]{:S(2)}) collective-permute-start(f32[112,4,64]{2,0,1:T(8,128)S(1)} %constant_dynamic-update-slice_fusion.15), channel_id=1, source_target_pairs={{0,4},{2,6},{4,0},{6,2},{1,5},{3,7},{5,1},{7,3},{8,12},{10,14},{12... | collective-permute-start | bytes 344072 | tf_op jit(solution)/shard_map/ppermute | solution.py:45
  86.9 21.0 %collective-permute-start.22 = (f32[112,4,64]{2,0,1:T(8,128)S(1)}, f32[112,4,64]{2,0,1:T(8,128)S(1)}, u32[]{:S(2)}, u32[]{:S(2)}) collective-permute-start(f32[112,4,64]{2,0,1:T(8,128)S(1)} %constant_dynamic-update-slice_fusion.15), channel_id=1, source_target_pairs={{0,2},{2,4},{4,6},{6,0},{1,3},{3,5},{5,7},{7,1},{8,10},{10,12},{12... | collective-permute-start | bytes 344072 | tf_op jit(solution)/shard_map/ppermute | solution.py:45
  87.6 16.3 %collective-permute-start.14 = (f32[32,6,128]{2,1,0:T(8,128)S(1)}, f32[32,6,128]{2,1,0:T(8,128)S(1)}, u32[]{:S(2)}, u32[]{:S(2)}) collective-permute-start(f32[32,6,128]{2,1,0:T(8,128)S(1)} %get-tuple-element.217), channel_id=1, source_target_pairs={{0,2},{2,4},{4,6},{1,3},{3,5},{5,7},{8,10},{10,12},{12,14},{9,11},... | collective-permute-start | bytes 294920 | tf_op jit(solution)/shard_map/ppermute | solution.py:36
  92.3 13.9 %collective-permute-start.15 = (f32[32,6,128]{2,1,0:T(8,128)S(1)}, f32[32,6,128]{2,1,0:T(8,128)S(1)}, u32[]{:S(2)}, u32[]{:S(2)}) collective-permute-start(f32[32,6,128]{2,1,0:T(8,128)S(1)} %get-tuple-element.218), channel_id=1, source_target_pairs={{2,0},{4,2},{6,4},{3,1},{5,3},{7,5},{10,8},{12,10},{14,12},{11,9},... | collective-permute-start | bytes 294920 | tf_op jit(solution)/shard_map/ppermute | solution.py:37
  127.8 1.3 collective-permute-start.34
  130.0 1.3 collective-permute-start.35
  132.2 1.3 collective-permute-start.36
  134.4 1.3 collective-permute-start.37
  (18 other events, 74.3 us)
where the time goes:
time: 140 us; the launch traced here: 139 us
  waiting for transfers between devices  58.3 us (42%)
  starting transfers between devices  35.9 us (26%)
  other arithmetic  22.6 us (16%)
  matrix products  11.7 us (8%)
  local copies, waits for them, and re-layouts  8.59 us (6%)
  between operations  2.31 us (2%)
    ppermute x24, waiting for transfers between devices, layer_halos(): got = lax.ppermute(jnp.where(first, tail, head), 'gz', [(0, 1), (1, 0)])  23.9 us
    ppermute x3, starting transfers between devices, extend_rows(): lo = lax.ppermute(a[:, -h:], 'gy', [(i, i + 1) for i in range(count - 1)])  12.8 us
    ppermute x3, waiting for transfers between devices, extend_rows(): lo = lax.ppermute(a[:, -h:], 'gy', [(i, i + 1) for i in range(count - 1)])  12.1 us
    ppermute x3, waiting for transfers between devices, extend_rows(): hi = lax.ppermute(a[:, :h], 'gy', [(i + 1, i) for i in range(count - 1)])  7.99 us
    ppermute x1, waiting for transfers between devices, extend_cols(): hi = lax.ppermute(a[:, :, :h], 'gx', [(i + 1, i) for i in range(count - 1)])  7.91 us
    ppermute x7, starting transfers between devices, gather_blocks(): lax.ppermute(a, axis, [(i, (i + s) % count) for i in range(count)])  7.83 us
    select_n x16, other arithmetic, sweep(): return jnp.where(inside, new, 0.0)  7.78 us
    dot_general x8, matrix products, rows(): return jnp.einsum('yr,zyx->zrx', pick(a.shape[1], parity), a, precision=HI)  5.71 us
  transfers between devices with their start and end apart: 39, of which 33 were waited for; matrix products, arithmetic and copies ran while one was open for 2% of the time, Pallas kernels for 0%

commit v1 on v0

--- a/solution.py
+++ b/solution.py
@@ -230,6 +230,9 @@
     lam = jnp.where(in_fine, OMEGA * src_e / dfine, 0.0)
     lam = smooth(lam, src_e, fine, dfine, in_fine, S0 - 1)
     b_mid = mean_four(src_e - operate(lam, fine))
+    coarse_all, b_mid = lax.optimization_barrier((coarse_all, b_mid))
+    coarse = tuple(coarse_all[i * layers : (i + 1) * layers] for i in range(7))
+    dcoarse = diagonal(coarse)
     e_mid = jnp.where(in_mid, OMEGA * b_mid / dmid, 0.0)
     e_mid = smooth(e_mid, b_mid, middle, dmid, in_mid, S1 - 1)
     hm = FINE_HALO // 2

time: 140 us -> 134 us (0.957)
  starting transfers between devices: 35.9 us -> 33.5 us
  other arithmetic: 22.6 us -> 20.4 us
    ppermute x7, waiting for transfers between devices: 2.46 us -> 15.3 us  [gather_blocks(): lax.ppermute(a, axis, [(i, (i + s) % count) for i in range(count)])]
    ppermute x3, waiting for transfers between devices: 12.1 us -> 1.98 us  [extend_rows(): lo = lax.ppermute(a[:, -h:], 'gy', [(i, i + 1) for i in range(count - 1)])]
    ppermute x3, starting transfers between devices: 12.8 us -> 10.1 us  [extend_rows(): lo = lax.ppermute(a[:, -h:], 'gy', [(i, i + 1) for i in range(count - 1)])]
    add x1, other arithmetic: 2.77 us -> 0.22 us  [diagonal(): return zlo + zhi + ylo + yhi + xlo + xhi + extra]
    ppermute x3, waiting for transfers between devices: 7.99 us -> 5.65 us  [extend_rows(): hi = lax.ppermute(a[:, :h], 'gy', [(i + 1, i) for i in range(count - 1)])]
    ppermute x24, waiting for transfers between devices: 23.9 us -> 22.3 us  [layer_halos(): got = lax.ppermute(jnp.where(first, tail, head), 'gz', [(0, 1), (1, 0)])]
    select_n x16 -> x17, other arithmetic: 7.78 us -> 7.86 us  [sweep(): return jnp.where(inside, new, 0.0)]
  transfers between devices with their start and end apart: 39 -> 39, of which waited for: 33 -> 30; matrix products, arithmetic and copies ran while one was open for 2% -> 13% of each run, Pallas kernels for 0% -> 0%
where the time goes in v1:
time: 134 us
  waiting for transfers between devices  57 us (43%)
  starting transfers between devices  33.5 us (25%)
  other arithmetic  20.4 us (15%)
  matrix products  12 us (9%)
  local copies, waits for them, and re-layouts  8.11 us (6%)
  between operations  2.4 us (2%)
    ppermute x24, waiting for transfers between devices, layer_halos(): got = lax.ppermute(jnp.where(first, tail, head), 'gz', [(0, 1), (1, 0)])  22.3 us
    ppermute x7, waiting for transfers between devices, gather_blocks(): lax.ppermute(a, axis, [(i, (i + s) % count) for i in range(count)])  15.3 us
    ppermute x3, starting transfers between devices, extend_rows(): lo = lax.ppermute(a[:, -h:], 'gy', [(i, i + 1) for i in range(count - 1)])  10.1 us
    ppermute x7, starting transfers between devices, gather_blocks(): lax.ppermute(a, axis, [(i, (i + s) % count) for i in range(count)])  8.34 us
    ppermute x1, waiting for transfers between devices, extend_cols(): hi = lax.ppermute(a[:, :, :h], 'gx', [(i + 1, i) for i in range(count - 1)])  7.91 us
    select_n x17, other arithmetic, sweep(): return jnp.where(inside, new, 0.0)  7.86 us
    dot_general x8, matrix products, rows(): return jnp.einsum('yr,zyx->zrx', pick(a.shape[1], parity), a, precision=HI)  5.85 us
    ppermute x3, waiting for transfers between devices, extend_rows(): hi = lax.ppermute(a[:, :h], 'gy', [(i + 1, i) for i in range(count - 1)])  5.65 us
  transfers between devices with their start and end apart: 39, of which 30 were waited for; matrix products, arithmetic and copies ran while one was open for 13% of the time, Pallas kernels for 0%

profile of v1, /device:TPU:0, one launch (start us, length us, event | category | flops | bytes accessed | tf_op | source)
XLA Modules:
  0.0 133.5 jit_solution(17642499450721682307)
XLA Ops:
  3.2 4.9 %collective-permute-start = (f32[34,16,64]{2,1,0:T(8,128)S(1)}, f32[34,16,64]{2,1,0:T(8,128)S(1)}, u32[]{:S(2)}, u32[]{:S(2)}) collective-permute-start(f32[34,16,64]{2,1,0:T(8,128)S(1)} %get-tuple-element.97), channel_id=1, source_target_pairs={{0,8},{8,16},{16,24},{1,9},{9,17},{17,25},{2,10},{10,18},{18,26},{... | collective-permute-start | bytes 417800 | tf_op jit(solution)/shard_map/ppermute | solution.py:52
  8.1 1.3 collective-permute-start.1
  10.0 3.9 %collective-permute-done = f32[34,16,64]{2,1,0:T(8,128)S(1)} collective-permute-done((f32[34,16,64]{2,1,0:T(8,128)S(1)}, f32[34,16,64]{2,1,0:T(8,128)S(1)}, u32[]{:S(2)}, u32[]{:S(2)}) %collective-permute-start) | collective-permute-done | bytes 139296 | tf_op jit(solution)/shard_map/ppermute | solution.py:52
  14.0 7.9 %collective-permute-done.1 = f32[34,16,64]{2,1,0:T(8,128)S(1)} collective-permute-done((f32[34,16,64]{2,1,0:T(8,128)S(1)}, f32[34,16,64]{2,1,0:T(8,128)S(1)}, u32[]{:S(2)}, u32[]{:S(2)}) %collective-permute-start.1) | collective-permute-done | bytes 139296 | tf_op jit(solution)/shard_map/ppermute | solution.py:53
  23.3 3.5 %collective-permute-start.2 = (f32[16,13,256]{2,1,0:T(8,128)S(1)}, f32[16,13,256]{2,1,0:T(8,128)S(1)}, u32[]{:S(2)}, u32[]{:S(2)}) collective-permute-start(f32[16,13,256]{2,1,0:T(8,128)S(1)} %get-tuple-element.67), channel_id=1, source_target_pairs={{0,2},{2,4},{4,6},{1,3},{3,5},{5,7},{8,10},{10,12},{12,14},{9,11},... | collective-permute-start | bytes 638984 | tf_op jit(solution)/shard_map/ppermute | solution.py:36
  26.8 1.3 collective-permute-start.3
  28.2 4.6 %collective-permute-start.4 = (f32[18,13,256]{2,1,0:T(8,128)S(1)}, f32[18,13,256]{2,1,0:T(8,128)S(1)}, u32[]{:S(2)}, u32[]{:S(2)}) collective-permute-start(f32[18,13,256]{2,1,0:T(8,128)S(1)} %get-tuple-element.95), channel_id=1, source_target_pairs={{0,2},{2,4},{4,6},{1,3},{3,5},{5,7},{8,10},{10,12},{12,14},{9,11},... | collective-permute-start | bytes 718856 | tf_op jit(solution)/shard_map/ppermute | solution.py:36
  32.8 1.3 collective-permute-start.5
  34.1 1.5 %collective-permute-done.3 = f32[16,13,256]{2,1,0:T(8,128)S(1)} collective-permute-done((f32[16,13,256]{2,1,0:T(8,128)S(1)}, f32[16,13,256]{2,1,0:T(8,128)S(1)}, u32[]{:S(2)}, u32[]{:S(2)}) %collective-permute-start.3) | collective-permute-done | bytes 213024 | tf_op jit(solution)/shard_map/ppermute | solution.py:37
  35.8 2.0 %collective-permute-done.4 = f32[18,13,256]{2,1,0:T(8,128)S(1)} collective-permute-done((f32[18,13,256]{2,1,0:T(8,128)S(1)}, f32[18,13,256]{2,1,0:T(8,128)S(1)}, u32[]{:S(2)}, u32[]{:S(2)}) %collective-permute-start.4) | collective-permute-done | bytes 239648 | tf_op jit(solution)/shard_map/ppermute | solution.py:36
  37.7 4.1 %collective-permute-done.5 = f32[18,13,256]{2,1,0:T(8,128)S(1)} collective-permute-done((f32[18,13,256]{2,1,0:T(8,128)S(1)}, f32[18,13,256]{2,1,0:T(8,128)S(1)}, u32[]{:S(2)}, u32[]{:S(2)}) %collective-permute-start.5) | collective-permute-done | bytes 239648 | tf_op jit(solution)/shard_map/ppermute | solution.py:37
  46.5 1.8 %fusion.378 = f32[112,256,20]{1,2,0:T(8,128)S(1)} fusion(f32[112,40,256]{2,1,0:T(8,128)S(1)} %fusion.53, s32[20]{0:T(128)S(1)} %iota_multiply_fusion.4), kind=kOutput, calls=%fused_computation.629 | convolution fusion | flops 275252000 | bytes 6881360 | tf_op jit(solution)/shard_map/yr,zyx->zrx/dot_general | solution.py:121
  48.3 1.9 %fusion.382 = f32[112,256,20]{1,2,0:T(8,128)S(1)} fusion(f32[112,40,256]{2,1,0:T(8,128)S(1)} %fusion.53, s32[20]{0:T(128)S(1)} %broadcast_add_fusion.7), kind=kOutput, calls=%fused_computation.631 | convolution fusion | flops 275252000 | bytes 6881360 | tf_op jit(solution)/shard_map/yr,zyx->zrx/dot_general | solution.py:121
  50.2 1.4 %copy_bitcast_fusion = (f32[112,20,256]{2,0,1:T(8,128)S(1)}, f32[112,20,256]{2,0,1:T(8,128)S(1)}) fusion(f32[112,256,20]{1,2,0:T(8,128)S(1)} %fusion.382, f32[112,256,20]{1,2,0:T(8,128)S(1)} %fusion.378), kind=kLoop, calls=%fused_computation.4 | loop fusion | bytes 9175040 | tf_op jit(solution)/shard_map/yr,zyx->zrx/transpose | solution.py:121
  51.6 2.2 %fusion = f32[224,20,256]{2,0,1:T(8,128)S(1)} fusion(f32[112,20,256]{2,0,1:T(8,128)S(1)} %get-tuple-element.252, f32[112,20,256]{2,0,1:T(8,128)S(1)} %get-tuple-element.253, s32[256]{0:T(256)S(1)} %get-tuple-element.255, s32[256]{0:T(256)S(1)} %get-tuple-element.254, pred[256]{0:T(512)(128)(4,1)S(1)} %iota_compare_fusion.8), kind=kOutput, calls=%fused_computation | convolution fusion | flops 3524493312 | bytes 9177344 | tf_op jit(solution)/shard_map/dot_general | solution.py:150
  56.2 1.6 %collective-permute-start.10 = (f32[112,4,64]{2,0,1:T(8,128)S(1)}, f32[112,4,64]{2,0,1:T(8,128)S(1)}, u32[]{:S(2)}, u32[]{:S(2)}) collective-permute-start(f32[112,4,64]{2,0,1:T(8,128)S(1)} %constant_dynamic-update-slice_fusion.7), channel_id=1, source_target_pairs={{0,6},{2,0},{4,2},{6,4},{1,7},{3,1},{5,3},{7,5},{8,14},{10,8},{12,... | collective-permute-start | bytes 344072 | tf_op jit(solution)/shard_map/ppermute | solution.py:45
  57.8 1.5 %collective-permute-start.11 = (f32[112,4,64]{2,0,1:T(8,128)S(1)}, f32[112,4,64]{2,0,1:T(8,128)S(1)}, u32[]{:S(2)}, u32[]{:S(2)}) collective-permute-start(f32[112,4,64]{2,0,1:T(8,128)S(1)} %constant_dynamic-update-slice_fusion.7), channel_id=1, source_target_pairs={{0,4},{2,6},{4,0},{6,2},{1,5},{3,7},{5,1},{7,3},{8,12},{10,14},{12... | collective-permute-start | bytes 344072 | tf_op jit(solution)/shard_map/ppermute | solution.py:45
  59.3 1.6 %collective-permute-start.12 = (f32[112,4,64]{2,0,1:T(8,128)S(1)}, f32[112,4,64]{2,0,1:T(8,128)S(1)}, u32[]{:S(2)}, u32[]{:S(2)}) collective-permute-start(f32[112,4,64]{2,0,1:T(8,128)S(1)} %constant_dynamic-update-slice_fusion.7), channel_id=1, source_target_pairs={{0,2},{2,4},{4,6},{6,0},{1,3},{3,5},{5,7},{7,1},{8,10},{10,12},{12... | collective-permute-start | bytes 344072 | tf_op jit(solution)/shard_map/ppermute | solution.py:45
  60.9 1.3 fusion.57
  65.8 14.1 %collective-permute-done.11 = f32[112,4,64]{2,0,1:T(8,128)S(1)} collective-permute-done((f32[112,4,64]{2,0,1:T(8,128)S(1)}, f32[112,4,64]{2,0,1:T(8,128)S(1)}, u32[]{:S(2)}, u32[]{:S(2)}) %collective-permute-start.11) | collective-permute-done | bytes 114720 | tf_op jit(solution)/shard_map/ppermute | solution.py:45
  94.8 1.5 %collective-permute-start.21 = (f32[16,4,64]{2,0,1:T(8,128)S(1)}, f32[16,4,64]{2,0,1:T(8,128)S(1)}, u32[]{:S(2)}, u32[]{:S(2)}) collective-permute-start(f32[16,4,64]{2,0,1:T(8,128)S(1)} %fusion.5), channel_id=1, source_target_pairs={{0,4},{2,6},{4,0},{6,2},{1,5},{3,7},{5,1},{7,3},{8,12},{10,14},{12... | collective-permute-start | bytes 49160 | tf_op jit(solution)/shard_map/ppermute | solution.py:45
  96.3 1.9 %collective-permute-start.22 = (f32[16,4,64]{2,0,1:T(8,128)S(1)}, f32[16,4,64]{2,0,1:T(8,128)S(1)}, u32[]{:S(2)}, u32[]{:S(2)}) collective-permute-start(f32[16,4,64]{2,0,1:T(8,128)S(1)} %fusion.5), channel_id=1, source_target_pairs={{0,2},{2,4},{4,6},{6,0},{1,3},{3,5},{5,7},{7,1},{8,10},{10,12},{12... | collective-permute-start | bytes 49160 | tf_op jit(solution)/shard_map/ppermute | solution.py:45
  98.3 2.0 %collective-permute-start.17 = (f32[32,6,128]{2,0,1:T(8,128)S(1)}, f32[32,6,128]{2,0,1:T(8,128)S(1)}, u32[]{:S(2)}, u32[]{:S(2)}) collective-permute-start(f32[32,6,128]{2,0,1:T(8,128)S(1)} %get-tuple-element.199), channel_id=1, source_target_pairs={{0,2},{2,4},{4,6},{1,3},{3,5},{5,7},{8,10},{10,12},{12,14},{9,11},... | collective-permute-start | bytes 294920 | tf_op jit(solution)/shard_map/ppermute | solution.py:36
  100.3 1.5 %collective-permute-start.18 = (f32[32,6,128]{2,0,1:T(8,128)S(1)}, f32[32,6,128]{2,0,1:T(8,128)S(1)}, u32[]{:S(2)}, u32[]{:S(2)}) collective-permute-start(f32[32,6,128]{2,0,1:T(8,128)S(1)} %get-tuple-element.200), channel_id=1, source_target_pairs={{2,0},{4,2},{6,4},{3,1},{5,3},{7,5},{10,8},{12,10},{14,12},{11,9},... | collective-permute-start | bytes 294920 | tf_op jit(solution)/shard_map/ppermute | solution.py:37
  (327 shorter events, 60.5 us)
Async XLA Ops:
  3.2 10.7 %collective-permute-start = (f32[34,16,64]{2,1,0:T(8,128)S(1)}, f32[34,16,64]{2,1,0:T(8,128)S(1)}, u32[]{:S(2)}, u32[]{:S(2)}) collective-permute-start(f32[34,16,64]{2,1,0:T(8,128)S(1)} %get-tuple-element.97), channel_id=1, source_target_pairs={{0,8},{8,16},{16,24},{1,9},{9,17},{17,25},{2,10},{10,18},{18,26},{... | collective-permute-start | bytes 417800 | tf_op jit(solution)/shard_map/ppermute | solution.py:52
  8.1 13.8 %collective-permute-start.1 = (f32[34,16,64]{2,1,0:T(8,128)S(1)}, f32[34,16,64]{2,1,0:T(8,128)S(1)}, u32[]{:S(2)}, u32[]{:S(2)}) collective-permute-start(f32[34,16,64]{2,1,0:T(8,128)S(1)} %get-tuple-element.98), channel_id=1, source_target_pairs={{8,0},{16,8},{24,16},{9,1},{17,9},{25,17},{10,2},{18,10},{26,18},{... | collective-permute-start | bytes 417800 | tf_op jit(solution)/shard_map/ppermute | solution.py:53
  23.3 10.8 %collective-permute-start.2 = (f32[16,13,256]{2,1,0:T(8,128)S(1)}, f32[16,13,256]{2,1,0:T(8,128)S(1)}, u32[]{:S(2)}, u32[]{:S(2)}) collective-permute-start(f32[16,13,256]{2,1,0:T(8,128)S(1)} %get-tuple-element.67), channel_id=1, source_target_pairs={{0,2},{2,4},{4,6},{1,3},{3,5},{5,7},{8,10},{10,12},{12,14},{9,11},... | collective-permute-start | bytes 638984 | tf_op jit(solution)/shard_map/ppermute | solution.py:36
  26.8 8.9 %collective-permute-start.3 = (f32[16,13,256]{2,1,0:T(8,128)S(1)}, f32[16,13,256]{2,1,0:T(8,128)S(1)}, u32[]{:S(2)}, u32[]{:S(2)}) collective-permute-start(f32[16,13,256]{2,1,0:T(8,128)S(1)} %get-tuple-element.68), channel_id=1, source_target_pairs={{2,0},{4,2},{6,4},{3,1},{5,3},{7,5},{10,8},{12,10},{14,12},{11,9},... | collective-permute-start | bytes 638984 | tf_op jit(solution)/shard_map/ppermute | solution.py:37
  28.2 9.5 %collective-permute-start.4 = (f32[18,13,256]{2,1,0:T(8,128)S(1)}, f32[18,13,256]{2,1,0:T(8,128)S(1)}, u32[]{:S(2)}, u32[]{:S(2)}) collective-permute-start(f32[18,13,256]{2,1,0:T(8,128)S(1)} %get-tuple-element.95), channel_id=1, source_target_pairs={{0,2},{2,4},{4,6},{1,3},{3,5},{5,7},{8,10},{10,12},{12,14},{9,11},... | collective-permute-start | bytes 718856 | tf_op jit(solution)/shard_map/ppermute | solution.py:36
  32.8 9.1 %collective-permute-start.5 = (f32[18,13,256]{2,1,0:T(8,128)S(1)}, f32[18,13,256]{2,1,0:T(8,128)S(1)}, u32[]{:S(2)}, u32[]{:S(2)}) collective-permute-start(f32[18,13,256]{2,1,0:T(8,128)S(1)} %get-tuple-element.96), channel_id=1, source_target_pairs={{2,0},{4,2},{6,4},{3,1},{5,3},{7,5},{10,8},{12,10},{14,12},{11,9},... | collective-permute-start | bytes 718856 | tf_op jit(solution)/shard_map/ppermute | solution.py:37
  42.6 1.3 collective-permute-start.6
  46.1 14.8 %collective-permute-start.7 = (f32[1,40,256]{2,1,0:T(8,128)S(1)}, f32[1,40,256]{2,1,0:T(8,128)S(1)}, u32[]{:S(2)}, u32[]{:S(2)}) collective-permute-start(f32[1,40,256]{2,1,0:T(8,128)S(1)} %slice_select_fusion.3), channel_id=1, source_target_pairs={{0,1},{1,0},{2,3},{3,2},{4,5},{5,4},{6,7},{7,6},{8,9},{9,8},{10,11... | collective-permute-start | bytes 122888 | tf_op jit(solution)/shard_map/ppermute | solution.py:26
  56.2 9.6 %collective-permute-start.10 = (f32[112,4,64]{2,0,1:T(8,128)S(1)}, f32[112,4,64]{2,0,1:T(8,128)S(1)}, u32[]{:S(2)}, u32[]{:S(2)}) collective-permute-start(f32[112,4,64]{2,0,1:T(8,128)S(1)} %constant_dynamic-update-slice_fusion.7), channel_id=1, source_target_pairs={{0,6},{2,0},{4,2},{6,4},{1,7},{3,1},{5,3},{7,5},{8,14},{10,8},{12,... | collective-permute-start | bytes 344072 | tf_op jit(solution)/shard_map/ppermute | solution.py:45
  57.8 22.1 %collective-permute-start.11 = (f32[112,4,64]{2,0,1:T(8,128)S(1)}, f32[112,4,64]{2,0,1:T(8,128)S(1)}, u32[]{:S(2)}, u32[]{:S(2)}) collective-permute-start(f32[112,4,64]{2,0,1:T(8,128)S(1)} %constant_dynamic-update-slice_fusion.7), channel_id=1, source_target_pairs={{0,4},{2,6},{4,0},{6,2},{1,5},{3,7},{5,1},{7,3},{8,12},{10,14},{12... | collective-permute-start | bytes 344072 | tf_op jit(solution)/shard_map/ppermute | solution.py:45
  59.3 20.6 %collective-permute-start.12 = (f32[112,4,64]{2,0,1:T(8,128)S(1)}, f32[112,4,64]{2,0,1:T(8,128)S(1)}, u32[]{:S(2)}, u32[]{:S(2)}) collective-permute-start(f32[112,4,64]{2,0,1:T(8,128)S(1)} %constant_dynamic-update-slice_fusion.7), channel_id=1, source_target_pairs={{0,2},{2,4},{4,6},{6,0},{1,3},{3,5},{5,7},{7,1},{8,10},{10,12},{12... | collective-permute-start | bytes 344072 | tf_op jit(solution)/shard_map/ppermute | solution.py:45
  62.6 1.3 collective-permute-start.8
  65.6 14.7 %collective-permute-start.9 = (f32[1,40,256]{2,1,0:T(8,128)S(1)}, f32[1,40,256]{2,1,0:T(8,128)S(1)}, u32[]{:S(2)}, u32[]{:S(2)}) collective-permute-start(f32[1,40,256]{2,1,0:T(8,128)S(1)} %slice_select_fusion.1), channel_id=1, source_target_pairs={{0,1},{1,0},{2,3},{3,2},{4,5},{5,4},{6,7},{7,6},{8,9},{9,8},{10,11... | collective-permute-start | bytes 122888 | tf_op jit(solution)/shard_map/ppermute | solution.py:26
  81.8 1.3 collective-permute-start.13
  91.8 1.2 collective-permute-start.19
  94.7 7.1 %collective-permute-start.20 = (f32[16,4,64]{2,0,1:T(8,128)S(1)}, f32[16,4,64]{2,0,1:T(8,128)S(1)}, u32[]{:S(2)}, u32[]{:S(2)}) collective-permute-start(f32[16,4,64]{2,0,1:T(8,128)S(1)} %fusion.5), channel_id=1, source_target_pairs={{0,6},{2,0},{4,2},{6,4},{1,7},{3,1},{5,3},{7,5},{8,14},{10,8},{12,... | collective-permute-start | bytes 49160 | tf_op jit(solution)/shard_map/ppermute | solution.py:45
  94.8 7.0 %collective-permute-start.21 = (f32[16,4,64]{2,0,1:T(8,128)S(1)}, f32[16,4,64]{2,0,1:T(8,128)S(1)}, u32[]{:S(2)}, u32[]{:S(2)}) collective-permute-start(f32[16,4,64]{2,0,1:T(8,128)S(1)} %fusion.5), channel_id=1, source_target_pairs={{0,4},{2,6},{4,0},{6,2},{1,5},{3,7},{5,1},{7,3},{8,12},{10,14},{12... | collective-permute-start | bytes 49160 | tf_op jit(solution)/shard_map/ppermute | solution.py:45
  96.3 5.7 %collective-permute-start.22 = (f32[16,4,64]{2,0,1:T(8,128)S(1)}, f32[16,4,64]{2,0,1:T(8,128)S(1)}, u32[]{:S(2)}, u32[]{:S(2)}) collective-permute-start(f32[16,4,64]{2,0,1:T(8,128)S(1)} %fusion.5), channel_id=1, source_target_pairs={{0,2},{2,4},{4,6},{6,0},{1,3},{3,5},{5,7},{7,1},{8,10},{10,12},{12... | collective-permute-start | bytes 49160 | tf_op jit(solution)/shard_map/ppermute | solution.py:45
  98.3 15.9 %collective-permute-start.17 = (f32[32,6,128]{2,0,1:T(8,128)S(1)}, f32[32,6,128]{2,0,1:T(8,128)S(1)}, u32[]{:S(2)}, u32[]{:S(2)}) collective-permute-start(f32[32,6,128]{2,0,1:T(8,128)S(1)} %get-tuple-element.199), channel_id=1, source_target_pairs={{0,2},{2,4},{4,6},{1,3},{3,5},{5,7},{8,10},{10,12},{12,14},{9,11},... | collective-permute-start | bytes 294920 | tf_op jit(solution)/shard_map/ppermute | solution.py:36
  100.3 13.9 %collective-permute-start.18 = (f32[32,6,128]{2,0,1:T(8,128)S(1)}, f32[32,6,128]{2,0,1:T(8,128)S(1)}, u32[]{:S(2)}, u32[]{:S(2)}) collective-permute-start(f32[32,6,128]{2,0,1:T(8,128)S(1)} %get-tuple-element.200), channel_id=1, source_target_pairs={{2,0},{4,2},{6,4},{3,1},{5,3},{7,5},{10,8},{12,10},{14,12},{11,9},... | collective-permute-start | bytes 294920 | tf_op jit(solution)/shard_map/ppermute | solution.py:37
  121.9 1.3 collective-permute-start.34
  124.2 1.3 collective-permute-start.35
  126.4 1.3 collective-permute-start.36
  128.6 1.3 collective-permute-start.37
  (18 other events, 74.3 us)

commit v2 on v1

--- a/solution.py
+++ b/solution.py
@@ -220,7 +220,8 @@
     middle = coarsen_stacked(fine)
     dmid = diagonal(middle)
     coarse_own = coarsen_stacked(crop_all(middle, FINE_HALO // 2, 0))
-    coarse_all = gather_blocks(jnp.concatenate(coarse_own, axis=0), "gy")
+    coarse_stack, src_e = lax.optimization_barrier((jnp.concatenate(coarse_own, axis=0), src_e))
+    coarse_all = gather_blocks(coarse_stack, "gy")
     coarse_all = jnp.concatenate([coarse_all[i] for i in range(coarse_all.shape[0])], axis=1)
     coarse = tuple(coarse_all[i * layers : (i + 1) * layers] for i in range(7))
     dcoarse = diagonal(coarse)

time: 134 us -> 134 us (level)
  starting transfers between devices: 33.5 us -> 39.7 us
  waiting for transfers between devices: 57 us -> 50.8 us
    ppermute x7, waiting for transfers between devices: 15.3 us -> 8.05 us  [gather_blocks(): lax.ppermute(a, axis, [(i, (i + s) % count) for i in range(count)])]
    ppermute x7, starting transfers between devices: 8.34 us -> 13.6 us  [gather_blocks(): lax.ppermute(a, axis, [(i, (i + s) % count) for i in range(count)])]
    slice x24 -> x23, local copies, waits for them, and re-layouts: 3.35 us -> 3.07 us  [neighbours(): xm = jnp.concatenate([zero_col, u[:, :, :-1]], axis=2)]
  transfers between devices with their start and end apart: 39 -> 39, of which waited for: 30 -> 31; matrix products, arithmetic and copies ran while one was open for 13% -> 7% of each run, Pallas kernels for 0% -> 0%
where the time goes in v2:
time: 134 us; the launch traced here: 133 us
  waiting for transfers between devices  50.8 us (38%)
  starting transfers between devices  39.7 us (30%)
  other arithmetic  20 us (15%)
  matrix products  11.9 us (9%)
  local copies, waits for them, and re-layouts  8.27 us (6%)
  between operations  2.44 us (2%)
    ppermute x24, waiting for transfers between devices, layer_halos(): got = lax.ppermute(jnp.where(first, tail, head), 'gz', [(0, 1), (1, 0)])  23.2 us
    ppermute x7, starting transfers between devices, gather_blocks(): lax.ppermute(a, axis, [(i, (i + s) % count) for i in range(count)])  13.6 us
    ppermute x3, starting transfers between devices, extend_rows(): lo = lax.ppermute(a[:, -h:], 'gy', [(i, i + 1) for i in range(count - 1)])  11.2 us
    ppermute x7, waiting for transfers between devices, gather_blocks(): lax.ppermute(a, axis, [(i, (i + s) % count) for i in range(count)])  8.05 us
    ppermute x1, waiting for transfers between devices, extend_cols(): hi = lax.ppermute(a[:, :, :h], 'gx', [(i + 1, i) for i in range(count - 1)])  7.91 us
    select_n x17, other arithmetic, sweep(): return jnp.where(inside, new, 0.0)  7.36 us
    dot_general x8, matrix products, rows(): return jnp.einsum('yr,zyx->zrx', pick(a.shape[1], parity), a, precision=HI)  5.92 us
    ppermute x3, waiting for transfers between devices, extend_rows(): hi = lax.ppermute(a[:, :h], 'gy', [(i + 1, i) for i in range(count - 1)])  5.65 us
  transfers between devices with their start and end apart: 39, of which 31 were waited for; matrix products, arithmetic and copies ran while one was open for 7% of the time, Pallas kernels for 0%

profile of v2, /device:TPU:0, one launch (start us, length us, event | category | flops | bytes accessed | tf_op | source)
XLA Modules:
  0.0 133.1 jit_solution(16290645648820864940)
XLA Ops:
  3.2 4.9 %collective-permute-start = (f32[34,16,64]{2,1,0:T(8,128)S(1)}, f32[34,16,64]{2,1,0:T(8,128)S(1)}, u32[]{:S(2)}, u32[]{:S(2)}) collective-permute-start(f32[34,16,64]{2,1,0:T(8,128)S(1)} %get-tuple-element.100), channel_id=1, source_target_pairs={{0,8},{8,16},{16,24},{1,9},{9,17},{17,25},{2,10},{10,18},{18,26},{... | collective-permute-start | bytes 417800 | tf_op jit(solution)/shard_map/ppermute | solution.py:52
  8.1 1.3 collective-permute-start.1
  10.1 3.9 %collective-permute-done = f32[34,16,64]{2,1,0:T(8,128)S(1)} collective-permute-done((f32[34,16,64]{2,1,0:T(8,128)S(1)}, f32[34,16,64]{2,1,0:T(8,128)S(1)}, u32[]{:S(2)}, u32[]{:S(2)}) %collective-permute-start) | collective-permute-done | bytes 139296 | tf_op jit(solution)/shard_map/ppermute | solution.py:52
  14.0 7.9 %collective-permute-done.1 = f32[34,16,64]{2,1,0:T(8,128)S(1)} collective-permute-done((f32[34,16,64]{2,1,0:T(8,128)S(1)}, f32[34,16,64]{2,1,0:T(8,128)S(1)}, u32[]{:S(2)}, u32[]{:S(2)}) %collective-permute-start.1) | collective-permute-done | bytes 139296 | tf_op jit(solution)/shard_map/ppermute | solution.py:53
  21.9 1.2 pad_maximum_fusion.4
  23.3 3.5 %collective-permute-start.5 = (f32[16,13,256]{2,1,0:T(8,128)S(1)}, f32[16,13,256]{2,1,0:T(8,128)S(1)}, u32[]{:S(2)}, u32[]{:S(2)}) collective-permute-start(f32[16,13,256]{2,1,0:T(8,128)S(1)} %get-tuple-element.68), channel_id=1, source_target_pairs={{0,2},{2,4},{4,6},{1,3},{3,5},{5,7},{8,10},{10,12},{12,14},{9,11},... | collective-permute-start | bytes 638984 | tf_op jit(solution)/shard_map/ppermute | solution.py:36
  26.8 1.3 collective-permute-start.6
  28.2 4.6 %collective-permute-start.2 = (f32[18,13,256]{2,1,0:T(8,128)S(1)}, f32[18,13,256]{2,1,0:T(8,128)S(1)}, u32[]{:S(2)}, u32[]{:S(2)}) collective-permute-start(f32[18,13,256]{2,1,0:T(8,128)S(1)} %get-tuple-element.98), channel_id=1, source_target_pairs={{0,2},{2,4},{4,6},{1,3},{3,5},{5,7},{8,10},{10,12},{12,14},{9,11},... | collective-permute-start | bytes 718856 | tf_op jit(solution)/shard_map/ppermute | solution.py:36
  32.8 1.3 collective-permute-start.3
  34.1 1.5 %collective-permute-done.6 = f32[16,13,256]{2,1,0:T(8,128)S(1)} collective-permute-done((f32[16,13,256]{2,1,0:T(8,128)S(1)}, f32[16,13,256]{2,1,0:T(8,128)S(1)}, u32[]{:S(2)}, u32[]{:S(2)}) %collective-permute-start.6) | collective-permute-done | bytes 213024 | tf_op jit(solution)/shard_map/ppermute | solution.py:37
  35.7 2.0 %collective-permute-done.2 = f32[18,13,256]{2,1,0:T(8,128)S(1)} collective-permute-done((f32[18,13,256]{2,1,0:T(8,128)S(1)}, f32[18,13,256]{2,1,0:T(8,128)S(1)}, u32[]{:S(2)}, u32[]{:S(2)}) %collective-permute-start.2) | collective-permute-done | bytes 239648 | tf_op jit(solution)/shard_map/ppermute | solution.py:36
  37.7 4.1 %collective-permute-done.3 = f32[18,13,256]{2,1,0:T(8,128)S(1)} collective-permute-done((f32[18,13,256]{2,1,0:T(8,128)S(1)}, f32[18,13,256]{2,1,0:T(8,128)S(1)}, u32[]{:S(2)}, u32[]{:S(2)}) %collective-permute-start.3) | collective-permute-done | bytes 239648 | tf_op jit(solution)/shard_map/ppermute | solution.py:37
  45.2 1.9 %fusion.381 = f32[112,256,20]{1,2,0:T(8,128)S(1)} fusion(f32[112,40,256]{2,1,0:T(8,128)S(1)} %fusion.53, s32[20]{0:T(128)S(1)} %broadcast_add_fusion.7), kind=kOutput, calls=%fused_computation.632 | convolution fusion | flops 275252000 | bytes 6881360 | tf_op jit(solution)/shard_map/yr,zyx->zrx/dot_general | solution.py:121
  47.2 1.9 %fusion.377 = f32[112,256,20]{1,2,0:T(8,128)S(1)} fusion(f32[112,40,256]{2,1,0:T(8,128)S(1)} %fusion.53, s32[20]{0:T(128)S(1)} %iota_multiply_fusion.4), kind=kOutput, calls=%fused_computation.630 | convolution fusion | flops 275252000 | bytes 6881360 | tf_op jit(solution)/shard_map/yr,zyx->zrx/dot_general | solution.py:121
  49.1 1.4 %copy_bitcast_fusion = (f32[112,20,256]{2,0,1:T(8,128)S(1)}, f32[112,20,256]{2,0,1:T(8,128)S(1)}) fusion(f32[112,256,20]{1,2,0:T(8,128)S(1)} %fusion.381, f32[112,256,20]{1,2,0:T(8,128)S(1)} %fusion.377), kind=kLoop, calls=%fused_computation.4 | loop fusion | bytes 9175040 | tf_op jit(solution)/shard_map/yr,zyx->zrx/transpose | solution.py:121
  50.5 2.2 %fusion = f32[224,20,256]{2,0,1:T(8,128)S(1)} fusion(f32[112,20,256]{2,0,1:T(8,128)S(1)} %get-tuple-element.256, f32[112,20,256]{2,0,1:T(8,128)S(1)} %get-tuple-element.257, s32[256]{0:T(256)S(1)} %get-tuple-element.259, s32[256]{0:T(256)S(1)} %get-tuple-element.258, pred[256]{0:T(512)(128)(4,1)S(1)} %iota_compare_fusion.8), kind=kOutput, calls=%fused_computation | convolution fusion | flops 3524493312 | bytes 9177344 | tf_op jit(solution)/shard_map/dot_general | solution.py:150
  54.9 1.6 %collective-permute-start.12 = (f32[112,4,64]{2,0,1:T(8,128)S(1)}, f32[112,4,64]{2,0,1:T(8,128)S(1)}, u32[]{:S(2)}, u32[]{:S(2)}) collective-permute-start(f32[112,4,64]{2,0,1:T(8,128)S(1)} %constant_dynamic-update-slice_fusion.7), channel_id=1, source_target_pairs={{0,2},{2,4},{4,6},{6,0},{1,3},{3,5},{5,7},{7,1},{8,10},{10,12},{12... | collective-permute-start | bytes 344072 | tf_op jit(solution)/shard_map/ppermute | solution.py:45
  57.6 2.8 %collective-permute-start.10 = (f32[112,4,64]{2,0,1:T(8,128)S(1)}, f32[112,4,64]{2,0,1:T(8,128)S(1)}, u32[]{:S(2)}, u32[]{:S(2)}) collective-permute-start(f32[112,4,64]{2,0,1:T(8,128)S(1)} %constant_dynamic-update-slice_fusion.7), channel_id=1, source_target_pairs={{0,6},{2,0},{4,2},{6,4},{1,7},{3,1},{5,3},{7,5},{8,14},{10,8},{12,... | collective-permute-start | bytes 344072 | tf_op jit(solution)/shard_map/ppermute | solution.py:45
  67.3 4.2 %collective-permute-done.10 = f32[112,4,64]{2,0,1:T(8,128)S(1)} collective-permute-done((f32[112,4,64]{2,0,1:T(8,128)S(1)}, f32[112,4,64]{2,0,1:T(8,128)S(1)}, u32[]{:S(2)}, u32[]{:S(2)}) %collective-permute-start.10) | collective-permute-done | bytes 114720 | tf_op jit(solution)/shard_map/ppermute | solution.py:45
  71.6 2.8 %collective-permute-done.11 = f32[112,4,64]{2,0,1:T(8,128)S(1)} collective-permute-done((f32[112,4,64]{2,0,1:T(8,128)S(1)}, f32[112,4,64]{2,0,1:T(8,128)S(1)}, u32[]{:S(2)}, u32[]{:S(2)}) %collective-permute-start.11) | collective-permute-done | bytes 114720 | tf_op jit(solution)/shard_map/ppermute | solution.py:45
  89.1 5.5 %collective-permute-start.22 = (f32[16,4,64]{2,0,1:T(8,128)S(1)}, f32[16,4,64]{2,0,1:T(8,128)S(1)}, u32[]{:S(2)}, u32[]{:S(2)}) collective-permute-start(f32[16,4,64]{2,0,1:T(8,128)S(1)} %fusion.5), channel_id=1, source_target_pairs={{0,2},{2,4},{4,6},{6,0},{1,3},{3,5},{5,7},{7,1},{8,10},{10,12},{12... | collective-permute-start | bytes 49160 | tf_op jit(solution)/shard_map/ppermute | solution.py:45
  94.5 1.6 %collective-permute-start.21 = (f32[16,4,64]{2,0,1:T(8,128)S(1)}, f32[16,4,64]{2,0,1:T(8,128)S(1)}, u32[]{:S(2)}, u32[]{:S(2)}) collective-permute-start(f32[16,4,64]{2,0,1:T(8,128)S(1)} %fusion.5), channel_id=1, source_target_pairs={{0,4},{2,6},{4,0},{6,2},{1,5},{3,7},{5,1},{7,3},{8,12},{10,14},{12... | collective-permute-start | bytes 49160 | tf_op jit(solution)/shard_map/ppermute | solution.py:45
  97.0 3.1 %collective-permute-start.17 = (f32[32,6,128]{2,0,1:T(8,128)S(1)}, f32[32,6,128]{2,0,1:T(8,128)S(1)}, u32[]{:S(2)}, u32[]{:S(2)}) collective-permute-start(f32[32,6,128]{2,0,1:T(8,128)S(1)} %get-tuple-element.202), channel_id=1, source_target_pairs={{0,2},{2,4},{4,6},{1,3},{3,5},{5,7},{8,10},{10,12},{12,14},{9,11},... | collective-permute-start | bytes 294920 | tf_op jit(solution)/shard_map/ppermute | solution.py:36
  100.1 1.3 collective-permute-start.18
  (331 shorter events, 62.7 us)
Async XLA Ops:
  3.2 10.7 %collective-permute-start = (f32[34,16,64]{2,1,0:T(8,128)S(1)}, f32[34,16,64]{2,1,0:T(8,128)S(1)}, u32[]{:S(2)}, u32[]{:S(2)}) collective-permute-start(f32[34,16,64]{2,1,0:T(8,128)S(1)} %get-tuple-element.100), channel_id=1, source_target_pairs={{0,8},{8,16},{16,24},{1,9},{9,17},{17,25},{2,10},{10,18},{18,26},{... | collective-permute-start | bytes 417800 | tf_op jit(solution)/shard_map/ppermute | solution.py:52
  8.1 13.8 %collective-permute-start.1 = (f32[34,16,64]{2,1,0:T(8,128)S(1)}, f32[34,16,64]{2,1,0:T(8,128)S(1)}, u32[]{:S(2)}, u32[]{:S(2)}) collective-permute-start(f32[34,16,64]{2,1,0:T(8,128)S(1)} %get-tuple-element.101), channel_id=1, source_target_pairs={{8,0},{16,8},{24,16},{9,1},{17,9},{25,17},{10,2},{18,10},{26,18},{... | collective-permute-start | bytes 417800 | tf_op jit(solution)/shard_map/ppermute | solution.py:53
  23.3 10.9 %collective-permute-start.5 = (f32[16,13,256]{2,1,0:T(8,128)S(1)}, f32[16,13,256]{2,1,0:T(8,128)S(1)}, u32[]{:S(2)}, u32[]{:S(2)}) collective-permute-start(f32[16,13,256]{2,1,0:T(8,128)S(1)} %get-tuple-element.68), channel_id=1, source_target_pairs={{0,2},{2,4},{4,6},{1,3},{3,5},{5,7},{8,10},{10,12},{12,14},{9,11},... | collective-permute-start | bytes 638984 | tf_op jit(solution)/shard_map/ppermute | solution.py:36
  26.8 8.9 %collective-permute-start.6 = (f32[16,13,256]{2,1,0:T(8,128)S(1)}, f32[16,13,256]{2,1,0:T(8,128)S(1)}, u32[]{:S(2)}, u32[]{:S(2)}) collective-permute-start(f32[16,13,256]{2,1,0:T(8,128)S(1)} %get-tuple-element.69), channel_id=1, source_target_pairs={{2,0},{4,2},{6,4},{3,1},{5,3},{7,5},{10,8},{12,10},{14,12},{11,9},... | collective-permute-start | bytes 638984 | tf_op jit(solution)/shard_map/ppermute | solution.py:37
  28.2 9.5 %collective-permute-start.2 = (f32[18,13,256]{2,1,0:T(8,128)S(1)}, f32[18,13,256]{2,1,0:T(8,128)S(1)}, u32[]{:S(2)}, u32[]{:S(2)}) collective-permute-start(f32[18,13,256]{2,1,0:T(8,128)S(1)} %get-tuple-element.98), channel_id=1, source_target_pairs={{0,2},{2,4},{4,6},{1,3},{3,5},{5,7},{8,10},{10,12},{12,14},{9,11},... | collective-permute-start | bytes 718856 | tf_op jit(solution)/shard_map/ppermute | solution.py:36
  32.8 9.1 %collective-permute-start.3 = (f32[18,13,256]{2,1,0:T(8,128)S(1)}, f32[18,13,256]{2,1,0:T(8,128)S(1)}, u32[]{:S(2)}, u32[]{:S(2)}) collective-permute-start(f32[18,13,256]{2,1,0:T(8,128)S(1)} %get-tuple-element.99), channel_id=1, source_target_pairs={{2,0},{4,2},{6,4},{3,1},{5,3},{7,5},{10,8},{12,10},{14,12},{11,9},... | collective-permute-start | bytes 718856 | tf_op jit(solution)/shard_map/ppermute | solution.py:37
  42.6 1.3 collective-permute-start.4
  54.9 19.5 %collective-permute-start.12 = (f32[112,4,64]{2,0,1:T(8,128)S(1)}, f32[112,4,64]{2,0,1:T(8,128)S(1)}, u32[]{:S(2)}, u32[]{:S(2)}) collective-permute-start(f32[112,4,64]{2,0,1:T(8,128)S(1)} %constant_dynamic-update-slice_fusion.7), channel_id=1, source_target_pairs={{0,2},{2,4},{4,6},{6,0},{1,3},{3,5},{5,7},{7,1},{8,10},{10,12},{12... | collective-permute-start | bytes 344072 | tf_op jit(solution)/shard_map/ppermute | solution.py:45
  56.5 17.9 %collective-permute-start.11 = (f32[112,4,64]{2,0,1:T(8,128)S(1)}, f32[112,4,64]{2,0,1:T(8,128)S(1)}, u32[]{:S(2)}, u32[]{:S(2)}) collective-permute-start(f32[112,4,64]{2,0,1:T(8,128)S(1)} %constant_dynamic-update-slice_fusion.7), channel_id=1, source_target_pairs={{0,4},{2,6},{4,0},{6,2},{1,5},{3,7},{5,1},{7,3},{8,12},{10,14},{12... | collective-permute-start | bytes 344072 | tf_op jit(solution)/shard_map/ppermute | solution.py:45
  57.6 14.0 %collective-permute-start.10 = (f32[112,4,64]{2,0,1:T(8,128)S(1)}, f32[112,4,64]{2,0,1:T(8,128)S(1)}, u32[]{:S(2)}, u32[]{:S(2)}) collective-permute-start(f32[112,4,64]{2,0,1:T(8,128)S(1)} %constant_dynamic-update-slice_fusion.7), channel_id=1, source_target_pairs={{0,6},{2,0},{4,2},{6,4},{1,7},{3,1},{5,3},{7,5},{8,14},{10,8},{12,... | collective-permute-start | bytes 344072 | tf_op jit(solution)/shard_map/ppermute | solution.py:45
  61.4 1.3 collective-permute-start.7
  64.2 1.3 collective-permute-start.8
  67.1 7.6 %collective-permute-start.9 = (f32[1,40,256]{2,1,0:T(8,128)S(1)}, f32[1,40,256]{2,1,0:T(8,128)S(1)}, u32[]{:S(2)}, u32[]{:S(2)}) collective-permute-start(f32[1,40,256]{2,1,0:T(8,128)S(1)} %slice_select_fusion.1), channel_id=1, source_target_pairs={{0,1},{1,0},{2,3},{3,2},{4,5},{5,4},{6,7},{7,6},{8,9},{9,8},{10,11... | collective-permute-start | bytes 122888 | tf_op jit(solution)/shard_map/ppermute | solution.py:26
  76.2 1.3 collective-permute-start.13
  81.1 1.2 collective-permute-start.14
  89.1 12.4 %collective-permute-start.22 = (f32[16,4,64]{2,0,1:T(8,128)S(1)}, f32[16,4,64]{2,0,1:T(8,128)S(1)}, u32[]{:S(2)}, u32[]{:S(2)}) collective-permute-start(f32[16,4,64]{2,0,1:T(8,128)S(1)} %fusion.5), channel_id=1, source_target_pairs={{0,2},{2,4},{4,6},{6,0},{1,3},{3,5},{5,7},{7,1},{8,10},{10,12},{12... | collective-permute-start | bytes 49160 | tf_op jit(solution)/shard_map/ppermute | solution.py:45
  94.5 6.9 %collective-permute-start.21 = (f32[16,4,64]{2,0,1:T(8,128)S(1)}, f32[16,4,64]{2,0,1:T(8,128)S(1)}, u32[]{:S(2)}, u32[]{:S(2)}) collective-permute-start(f32[16,4,64]{2,0,1:T(8,128)S(1)} %fusion.5), channel_id=1, source_target_pairs={{0,4},{2,6},{4,0},{6,2},{1,5},{3,7},{5,1},{7,3},{8,12},{10,14},{12... | collective-permute-start | bytes 49160 | tf_op jit(solution)/shard_map/ppermute | solution.py:45
  96.1 5.3 %collective-permute-start.20 = (f32[16,4,64]{2,0,1:T(8,128)S(1)}, f32[16,4,64]{2,0,1:T(8,128)S(1)}, u32[]{:S(2)}, u32[]{:S(2)}) collective-permute-start(f32[16,4,64]{2,0,1:T(8,128)S(1)} %fusion.5), channel_id=1, source_target_pairs={{0,6},{2,0},{4,2},{6,4},{1,7},{3,1},{5,3},{7,5},{8,14},{10,8},{12,... | collective-permute-start | bytes 49160 | tf_op jit(solution)/shard_map/ppermute | solution.py:45
  97.0 16.6 %collective-permute-start.17 = (f32[32,6,128]{2,0,1:T(8,128)S(1)}, f32[32,6,128]{2,0,1:T(8,128)S(1)}, u32[]{:S(2)}, u32[]{:S(2)}) collective-permute-start(f32[32,6,128]{2,0,1:T(8,128)S(1)} %get-tuple-element.202), channel_id=1, source_target_pairs={{0,2},{2,4},{4,6},{1,3},{3,5},{5,7},{8,10},{10,12},{12,14},{9,11},... | collective-permute-start | bytes 294920 | tf_op jit(solution)/shard_map/ppermute | solution.py:36
  100.1 13.5 %collective-permute-start.18 = (f32[32,6,128]{2,0,1:T(8,128)S(1)}, f32[32,6,128]{2,0,1:T(8,128)S(1)}, u32[]{:S(2)}, u32[]{:S(2)}) collective-permute-start(f32[32,6,128]{2,0,1:T(8,128)S(1)} %get-tuple-element.203), channel_id=1, source_target_pairs={{2,0},{4,2},{6,4},{3,1},{5,3},{7,5},{10,8},{12,10},{14,12},{11,9},... | collective-permute-start | bytes 294920 | tf_op jit(solution)/shard_map/ppermute | solution.py:37
  121.4 1.3 collective-permute-start.34
  123.5 1.3 collective-permute-start.35
  125.6 1.3 collective-permute-start.36
  127.9 1.3 collective-permute-start.37
  (20 other events, 166.6 us)

commit v3 on v2

--- a/solution.py
+++ b/solution.py
@@ -232,6 +232,7 @@
     lam = smooth(lam, src_e, fine, dfine, in_fine, S0 - 1)
     b_mid = mean_four(src_e - operate(lam, fine))
     coarse_all, b_mid = lax.optimization_barrier((coarse_all, b_mid))
+    b_mid_post = extend_rows(crop(b_mid, FINE_HALO // 2, 0), MID_HALO)
     coarse = tuple(coarse_all[i * layers : (i + 1) * layers] for i in range(7))
     dcoarse = diagonal(coarse)
     e_mid = jnp.where(in_mid, OMEGA * b_mid / dmid, 0.0)
@@ -244,10 +245,8 @@
     e_low = jnp.where(ones, OMEGA * b_low / dcoarse, 0.0)
     e_low = smooth(e_low, b_low, coarse, dcoarse, ones, S2 - 1)
 
-    pair = jnp.concatenate([crop(e_mid, hm, 0), crop(b_mid, hm, 0)], axis=0)
-    pair = extend_rows(pair, MID_HALO)
-    e_mid = pair[:layers]
-    b_mid = pair[layers:]
+    e_mid = extend_rows(crop(e_mid, hm, 0), MID_HALO)
+    b_mid = b_mid_post
     low_rows = own_rows // 4
     ch = MID_HALO // 2
     padded = jnp.pad(e_low, ((0, 0), (ch, ch), (0, 0)))

time: 134 us -> 142 us (1.060)
  starting transfers between devices: 39.7 us -> 47.2 us
    ppermute x3 -> x4, starting transfers between devices: 11.2 us -> 19.9 us  [extend_rows(): lo = lax.ppermute(a[:, -h:], 'gy', [(i, i + 1) for i in range(count - 1)])]
    ppermute x7, waiting for transfers between devices: 8.05 us -> 11 us  [gather_blocks(): lax.ppermute(a, axis, [(i, (i + s) % count) for i in range(count)])]
    ppermute x7, starting transfers between devices: 13.6 us -> 11.2 us  [gather_blocks(): lax.ppermute(a, axis, [(i, (i + s) % count) for i in range(count)])]
    ppermute x24, waiting for transfers between devices: 23.2 us -> 21.3 us  [layer_halos(): got = lax.ppermute(jnp.where(first, tail, head), 'gz', [(0, 1), (1, 0)])]
    ppermute x3 -> x4, starting transfers between devices: 3.88 us -> 5.17 us  [extend_rows(): hi = lax.ppermute(a[:, :h], 'gy', [(i + 1, i) for i in range(count - 1)])]
    select_n x17 -> x18, other arithmetic: 7.36 us -> 7.81 us  [sweep(): return jnp.where(inside, new, 0.0)]
    ppermute x3 -> x4, waiting for transfers between devices: 5.65 us -> 5.65 us  [extend_rows(): hi = lax.ppermute(a[:, :h], 'gy', [(i + 1, i) for i in range(count - 1)])]
  transfers between devices with their start and end apart: 39 -> 41, of which waited for: 31 -> 30; matrix products, arithmetic and copies ran while one was open for 7% -> 8% of each run, Pallas kernels for 0% -> 0%
where the time goes in v3:
time: 142 us
  waiting for transfers between devices  51.9 us (37%)
  starting transfers between devices  47.2 us (33%)
  other arithmetic  20.2 us (14%)
  matrix products  11.9 us (8%)
  local copies, waits for them, and re-layouts  8.29 us (6%)
  between operations  2.46 us (2%)
    ppermute x24, waiting for transfers between devices, layer_halos(): got = lax.ppermute(jnp.where(first, tail, head), 'gz', [(0, 1), (1, 0)])  21.3 us
    ppermute x4, starting transfers between devices, extend_rows(): lo = lax.ppermute(a[:, -h:], 'gy', [(i, i + 1) for i in range(count - 1)])  19.9 us
    ppermute x7, starting transfers between devices, gather_blocks(): lax.ppermute(a, axis, [(i, (i + s) % count) for i in range(count)])  11.2 us
    ppermute x7, waiting for transfers between devices, gather_blocks(): lax.ppermute(a, axis, [(i, (i + s) % count) for i in range(count)])  11 us
    ppermute x1, waiting for transfers between devices, extend_cols(): hi = lax.ppermute(a[:, :, :h], 'gx', [(i + 1, i) for i in range(count - 1)])  7.91 us
    select_n x18, other arithmetic, sweep(): return jnp.where(inside, new, 0.0)  7.81 us
    dot_general x8, matrix products, rows(): return jnp.einsum('yr,zyx->zrx', pick(a.shape[1], parity), a, precision=HI)  5.92 us
    ppermute x4, waiting for transfers between devices, extend_rows(): hi = lax.ppermute(a[:, :h], 'gy', [(i + 1, i) for i in range(count - 1)])  5.65 us
  transfers between devices with their start and end apart: 41, of which 30 were waited for; matrix products, arithmetic and copies ran while one was open for 8% of the time, Pallas kernels for 0%

profile of v3, /device:TPU:0, one launch (start us, length us, event | category | flops | bytes accessed | tf_op | source)
XLA Modules:
  0.0 141.9 jit_solution(9575719142501776807)
XLA Ops:
  3.2 4.9 %collective-permute-start = (f32[34,16,64]{2,1,0:T(8,128)S(1)}, f32[34,16,64]{2,1,0:T(8,128)S(1)}, u32[]{:S(2)}, u32[]{:S(2)}) collective-permute-start(f32[34,16,64]{2,1,0:T(8,128)S(1)} %get-tuple-element.98), channel_id=1, source_target_pairs={{0,8},{8,16},{16,24},{1,9},{9,17},{17,25},{2,10},{10,18},{18,26},{... | collective-permute-start | bytes 417800 | tf_op jit(solution)/shard_map/ppermute | solution.py:52
  8.1 1.3 collective-permute-start.1
  10.1 3.9 %collective-permute-done = f32[34,16,64]{2,1,0:T(8,128)S(1)} collective-permute-done((f32[34,16,64]{2,1,0:T(8,128)S(1)}, f32[34,16,64]{2,1,0:T(8,128)S(1)}, u32[]{:S(2)}, u32[]{:S(2)}) %collective-permute-start) | collective-permute-done | bytes 139296 | tf_op jit(solution)/shard_map/ppermute | solution.py:52
  14.0 7.9 %collective-permute-done.1 = f32[34,16,64]{2,1,0:T(8,128)S(1)} collective-permute-done((f32[34,16,64]{2,1,0:T(8,128)S(1)}, f32[34,16,64]{2,1,0:T(8,128)S(1)}, u32[]{:S(2)}, u32[]{:S(2)}) %collective-permute-start.1) | collective-permute-done | bytes 139296 | tf_op jit(solution)/shard_map/ppermute | solution.py:53
  23.3 3.5 %collective-permute-start.5 = (f32[16,13,256]{2,1,0:T(8,128)S(1)}, f32[16,13,256]{2,1,0:T(8,128)S(1)}, u32[]{:S(2)}, u32[]{:S(2)}) collective-permute-start(f32[16,13,256]{2,1,0:T(8,128)S(1)} %get-tuple-element.68), channel_id=1, source_target_pairs={{0,2},{2,4},{4,6},{1,3},{3,5},{5,7},{8,10},{10,12},{12,14},{9,11},... | collective-permute-start | bytes 638984 | tf_op jit(solution)/shard_map/ppermute | solution.py:36
  26.8 1.3 collective-permute-start.6
  28.2 4.6 %collective-permute-start.2 = (f32[18,13,256]{2,1,0:T(8,128)S(1)}, f32[18,13,256]{2,1,0:T(8,128)S(1)}, u32[]{:S(2)}, u32[]{:S(2)}) collective-permute-start(f32[18,13,256]{2,1,0:T(8,128)S(1)} %get-tuple-element.96), channel_id=1, source_target_pairs={{0,2},{2,4},{4,6},{1,3},{3,5},{5,7},{8,10},{10,12},{12,14},{9,11},... | collective-permute-start | bytes 718856 | tf_op jit(solution)/shard_map/ppermute | solution.py:36
  32.8 1.3 collective-permute-start.3
  34.1 1.5 %collective-permute-done.6 = f32[16,13,256]{2,1,0:T(8,128)S(1)} collective-permute-done((f32[16,13,256]{2,1,0:T(8,128)S(1)}, f32[16,13,256]{2,1,0:T(8,128)S(1)}, u32[]{:S(2)}, u32[]{:S(2)}) %collective-permute-start.6) | collective-permute-done | bytes 213024 | tf_op jit(solution)/shard_map/ppermute | solution.py:37
  35.7 2.0 %collective-permute-done.2 = f32[18,13,256]{2,1,0:T(8,128)S(1)} collective-permute-done((f32[18,13,256]{2,1,0:T(8,128)S(1)}, f32[18,13,256]{2,1,0:T(8,128)S(1)}, u32[]{:S(2)}, u32[]{:S(2)}) %collective-permute-start.2) | collective-permute-done | bytes 239648 | tf_op jit(solution)/shard_map/ppermute | solution.py:36
  37.7 4.1 %collective-permute-done.3 = f32[18,13,256]{2,1,0:T(8,128)S(1)} collective-permute-done((f32[18,13,256]{2,1,0:T(8,128)S(1)}, f32[18,13,256]{2,1,0:T(8,128)S(1)}, u32[]{:S(2)}, u32[]{:S(2)}) %collective-permute-start.3) | collective-permute-done | bytes 239648 | tf_op jit(solution)/shard_map/ppermute | solution.py:37
  45.2 1.9 %fusion.380 = f32[112,256,20]{1,2,0:T(8,128)S(1)} fusion(f32[112,40,256]{2,1,0:T(8,128)S(1)} %fusion.53, s32[20]{0:T(128)S(1)} %broadcast_add_fusion.7), kind=kOutput, calls=%fused_computation.628 | convolution fusion | flops 275252000 | bytes 6881360 | tf_op jit(solution)/shard_map/yr,zyx->zrx/dot_general | solution.py:121
  47.2 1.9 %fusion.376 = f32[112,256,20]{1,2,0:T(8,128)S(1)} fusion(f32[112,40,256]{2,1,0:T(8,128)S(1)} %fusion.53, s32[20]{0:T(128)S(1)} %iota_multiply_fusion.4), kind=kOutput, calls=%fused_computation.626 | convolution fusion | flops 275252000 | bytes 6881360 | tf_op jit(solution)/shard_map/yr,zyx->zrx/dot_general | solution.py:121
  49.1 1.4 copy_bitcast_fusion
  50.5 2.2 %fusion = f32[224,20,256]{2,0,1:T(8,128)S(1)} fusion(f32[112,20,256]{2,0,1:T(8,128)S(1)} %get-tuple-element.254, f32[112,20,256]{2,0,1:T(8,128)S(1)} %get-tuple-element.255, s32[256]{0:T(256)S(1)} %get-tuple-element.257, s32[256]{0:T(256)S(1)} %get-tuple-element.256, pred[256]{0:T(512)(128)(4,1)S(1)} %iota_compare_fusion.8), kind=kOutput, calls=%fused_computation | convolution fusion | flops 3524493312 | bytes 9177344 | tf_op jit(solution)/shard_map/dot_general | solution.py:150
  54.9 1.6 %collective-permute-start.12 = (f32[112,4,64]{2,0,1:T(8,128)S(1)}, f32[112,4,64]{2,0,1:T(8,128)S(1)}, u32[]{:S(2)}, u32[]{:S(2)}) collective-permute-start(f32[112,4,64]{2,0,1:T(8,128)S(1)} %constant_dynamic-update-slice_fusion.7), channel_id=1, source_target_pairs={{0,2},{2,4},{4,6},{6,0},{1,3},{3,5},{5,7},{7,1},{8,10},{10,12},{12... | collective-permute-start | bytes 344072 | tf_op jit(solution)/shard_map/ppermute | solution.py:45
  57.6 2.8 %collective-permute-start.10 = (f32[112,4,64]{2,0,1:T(8,128)S(1)}, f32[112,4,64]{2,0,1:T(8,128)S(1)}, u32[]{:S(2)}, u32[]{:S(2)}) collective-permute-start(f32[112,4,64]{2,0,1:T(8,128)S(1)} %constant_dynamic-update-slice_fusion.7), channel_id=1, source_target_pairs={{0,6},{2,0},{4,2},{6,4},{1,7},{3,1},{5,3},{7,5},{8,14},{10,8},{12,... | collective-permute-start | bytes 344072 | tf_op jit(solution)/shard_map/ppermute | solution.py:45
  67.3 4.2 %collective-permute-done.10 = f32[112,4,64]{2,0,1:T(8,128)S(1)} collective-permute-done((f32[112,4,64]{2,0,1:T(8,128)S(1)}, f32[112,4,64]{2,0,1:T(8,128)S(1)}, u32[]{:S(2)}, u32[]{:S(2)}) %collective-permute-start.10) | collective-permute-done | bytes 114720 | tf_op jit(solution)/shard_map/ppermute | solution.py:45
  71.6 2.8 %collective-permute-done.11 = f32[112,4,64]{2,0,1:T(8,128)S(1)} collective-permute-done((f32[112,4,64]{2,0,1:T(8,128)S(1)}, f32[112,4,64]{2,0,1:T(8,128)S(1)}, u32[]{:S(2)}, u32[]{:S(2)}) %collective-permute-start.11) | collective-permute-done | bytes 114720 | tf_op jit(solution)/shard_map/ppermute | solution.py:45
  81.3 7.3 %collective-permute-start.30 = (f32[16,6,128]{2,0,1:T(8,128)S(1)}, f32[16,6,128]{2,0,1:T(8,128)S(1)}, u32[]{:S(2)}, u32[]{:S(2)}) collective-permute-start(f32[16,6,128]{2,0,1:T(8,128)S(1)} %get-tuple-element.122), channel_id=1, source_target_pairs={{0,2},{2,4},{4,6},{1,3},{3,5},{5,7},{8,10},{10,12},{12,14},{9,11},... | collective-permute-start | bytes 147464 | tf_op jit(solution)/shard_map/ppermute | solution.py:36
  94.1 4.5 %collective-permute-start.17 = (f32[16,6,128]{2,0,1:T(8,128)S(1)}, f32[16,6,128]{2,0,1:T(8,128)S(1)}, u32[]{:S(2)}, u32[]{:S(2)}) collective-permute-start(f32[16,6,128]{2,0,1:T(8,128)S(1)} %get-tuple-element.142), channel_id=1, source_target_pairs={{0,2},{2,4},{4,6},{1,3},{3,5},{5,7},{8,10},{10,12},{12,14},{9,11},... | collective-permute-start | bytes 147464 | tf_op jit(solution)/shard_map/ppermute | solution.py:36
  101.6 2.9 %collective-permute-start.22 = (f32[16,4,64]{2,0,1:T(8,128)S(1)}, f32[16,4,64]{2,0,1:T(8,128)S(1)}, u32[]{:S(2)}, u32[]{:S(2)}) collective-permute-start(f32[16,4,64]{2,0,1:T(8,128)S(1)} %fusion.5), channel_id=1, source_target_pairs={{0,2},{2,4},{4,6},{6,0},{1,3},{3,5},{5,7},{7,1},{8,10},{10,12},{12... | collective-permute-start | bytes 49160 | tf_op jit(solution)/shard_map/ppermute | solution.py:45
  104.6 1.6 %collective-permute-start.21 = (f32[16,4,64]{2,0,1:T(8,128)S(1)}, f32[16,4,64]{2,0,1:T(8,128)S(1)}, u32[]{:S(2)}, u32[]{:S(2)}) collective-permute-start(f32[16,4,64]{2,0,1:T(8,128)S(1)} %fusion.5), channel_id=1, source_target_pairs={{0,4},{2,6},{4,0},{6,2},{1,5},{3,7},{5,1},{7,3},{8,12},{10,14},{12... | collective-permute-start | bytes 49160 | tf_op jit(solution)/shard_map/ppermute | solution.py:45
  107.1 3.0 %collective-permute-done.20 = f32[16,4,64]{2,0,1:T(8,128)S(1)} collective-permute-done((f32[16,4,64]{2,0,1:T(8,128)S(1)}, f32[16,4,64]{2,0,1:T(8,128)S(1)}, u32[]{:S(2)}, u32[]{:S(2)}) %collective-permute-start.20) | collective-permute-done | bytes 16416 | tf_op jit(solution)/shard_map/ppermute | solution.py:45
  (337 shorter events, 64.8 us)
Async XLA Ops:
  3.2 10.7 %collective-permute-start = (f32[34,16,64]{2,1,0:T(8,128)S(1)}, f32[34,16,64]{2,1,0:T(8,128)S(1)}, u32[]{:S(2)}, u32[]{:S(2)}) collective-permute-start(f32[34,16,64]{2,1,0:T(8,128)S(1)} %get-tuple-element.98), channel_id=1, source_target_pairs={{0,8},{8,16},{16,24},{1,9},{9,17},{17,25},{2,10},{10,18},{18,26},{... | collective-permute-start | bytes 417800 | tf_op jit(solution)/shard_map/ppermute | solution.py:52
  8.1 13.8 %collective-permute-start.1 = (f32[34,16,64]{2,1,0:T(8,128)S(1)}, f32[34,16,64]{2,1,0:T(8,128)S(1)}, u32[]{:S(2)}, u32[]{:S(2)}) collective-permute-start(f32[34,16,64]{2,1,0:T(8,128)S(1)} %get-tuple-element.99), channel_id=1, source_target_pairs={{8,0},{16,8},{24,16},{9,1},{17,9},{25,17},{10,2},{18,10},{26,18},{... | collective-permute-start | bytes 417800 | tf_op jit(solution)/shard_map/ppermute | solution.py:53
  23.3 10.9 %collective-permute-start.5 = (f32[16,13,256]{2,1,0:T(8,128)S(1)}, f32[16,13,256]{2,1,0:T(8,128)S(1)}, u32[]{:S(2)}, u32[]{:S(2)}) collective-permute-start(f32[16,13,256]{2,1,0:T(8,128)S(1)} %get-tuple-element.68), channel_id=1, source_target_pairs={{0,2},{2,4},{4,6},{1,3},{3,5},{5,7},{8,10},{10,12},{12,14},{9,11},... | collective-permute-start | bytes 638984 | tf_op jit(solution)/shard_map/ppermute | solution.py:36
  26.8 8.9 %collective-permute-start.6 = (f32[16,13,256]{2,1,0:T(8,128)S(1)}, f32[16,13,256]{2,1,0:T(8,128)S(1)}, u32[]{:S(2)}, u32[]{:S(2)}) collective-permute-start(f32[16,13,256]{2,1,0:T(8,128)S(1)} %get-tuple-element.69), channel_id=1, source_target_pairs={{2,0},{4,2},{6,4},{3,1},{5,3},{7,5},{10,8},{12,10},{14,12},{11,9},... | collective-permute-start | bytes 638984 | tf_op jit(solution)/shard_map/ppermute | solution.py:37
  28.2 9.5 %collective-permute-start.2 = (f32[18,13,256]{2,1,0:T(8,128)S(1)}, f32[18,13,256]{2,1,0:T(8,128)S(1)}, u32[]{:S(2)}, u32[]{:S(2)}) collective-permute-start(f32[18,13,256]{2,1,0:T(8,128)S(1)} %get-tuple-element.96), channel_id=1, source_target_pairs={{0,2},{2,4},{4,6},{1,3},{3,5},{5,7},{8,10},{10,12},{12,14},{9,11},... | collective-permute-start | bytes 718856 | tf_op jit(solution)/shard_map/ppermute | solution.py:36
  32.8 9.1 %collective-permute-start.3 = (f32[18,13,256]{2,1,0:T(8,128)S(1)}, f32[18,13,256]{2,1,0:T(8,128)S(1)}, u32[]{:S(2)}, u32[]{:S(2)}) collective-permute-start(f32[18,13,256]{2,1,0:T(8,128)S(1)} %get-tuple-element.97), channel_id=1, source_target_pairs={{2,0},{4,2},{6,4},{3,1},{5,3},{7,5},{10,8},{12,10},{14,12},{11,9},... | collective-permute-start | bytes 718856 | tf_op jit(solution)/shard_map/ppermute | solution.py:37
  42.6 1.3 collective-permute-start.4
  54.9 19.5 %collective-permute-start.12 = (f32[112,4,64]{2,0,1:T(8,128)S(1)}, f32[112,4,64]{2,0,1:T(8,128)S(1)}, u32[]{:S(2)}, u32[]{:S(2)}) collective-permute-start(f32[112,4,64]{2,0,1:T(8,128)S(1)} %constant_dynamic-update-slice_fusion.7), channel_id=1, source_target_pairs={{0,2},{2,4},{4,6},{6,0},{1,3},{3,5},{5,7},{7,1},{8,10},{10,12},{12... | collective-permute-start | bytes 344072 | tf_op jit(solution)/shard_map/ppermute | solution.py:45
  56.5 17.9 %collective-permute-start.11 = (f32[112,4,64]{2,0,1:T(8,128)S(1)}, f32[112,4,64]{2,0,1:T(8,128)S(1)}, u32[]{:S(2)}, u32[]{:S(2)}) collective-permute-start(f32[112,4,64]{2,0,1:T(8,128)S(1)} %constant_dynamic-update-slice_fusion.7), channel_id=1, source_target_pairs={{0,4},{2,6},{4,0},{6,2},{1,5},{3,7},{5,1},{7,3},{8,12},{10,14},{12... | collective-permute-start | bytes 344072 | tf_op jit(solution)/shard_map/ppermute | solution.py:45
  57.6 14.0 %collective-permute-start.10 = (f32[112,4,64]{2,0,1:T(8,128)S(1)}, f32[112,4,64]{2,0,1:T(8,128)S(1)}, u32[]{:S(2)}, u32[]{:S(2)}) collective-permute-start(f32[112,4,64]{2,0,1:T(8,128)S(1)} %constant_dynamic-update-slice_fusion.7), channel_id=1, source_target_pairs={{0,6},{2,0},{4,2},{6,4},{1,7},{3,1},{5,3},{7,5},{8,14},{10,8},{12,... | collective-permute-start | bytes 344072 | tf_op jit(solution)/shard_map/ppermute | solution.py:45
  61.4 1.3 collective-permute-start.7
  64.2 1.3 collective-permute-start.8
  67.1 7.6 %collective-permute-start.9 = (f32[1,40,256]{2,1,0:T(8,128)S(1)}, f32[1,40,256]{2,1,0:T(8,128)S(1)}, u32[]{:S(2)}, u32[]{:S(2)}) collective-permute-start(f32[1,40,256]{2,1,0:T(8,128)S(1)} %slice_select_fusion.1), channel_id=1, source_target_pairs={{0,1},{1,0},{2,3},{3,2},{4,5},{5,4},{6,7},{7,6},{8,9},{9,8},{10,11... | collective-permute-start | bytes 122888 | tf_op jit(solution)/shard_map/ppermute | solution.py:26
  76.2 1.3 collective-permute-start.13
  81.1 8.9 %collective-permute-start.14 = (f32[1,20,128]{2,0,1:T(1,128)S(1)}, f32[1,20,128]{2,0,1:T(1,128)S(1)}, u32[]{:S(2)}, u32[]{:S(2)}) collective-permute-start(f32[1,20,128]{2,0,1:T(1,128)S(1)} %broadcast_select_fusion.33), channel_id=1, source_target_pairs={{0,1},{1,0},{2,3},{3,2},{4,5},{5,4},{6,7},{7,6},{8,9},{9,8},{10,11... | collective-permute-start | bytes 30728 | tf_op jit(solution)/shard_map/ppermute | solution.py:26
  81.3 23.2 %collective-permute-start.30 = (f32[16,6,128]{2,0,1:T(8,128)S(1)}, f32[16,6,128]{2,0,1:T(8,128)S(1)}, u32[]{:S(2)}, u32[]{:S(2)}) collective-permute-start(f32[16,6,128]{2,0,1:T(8,128)S(1)} %get-tuple-element.122), channel_id=1, source_target_pairs={{0,2},{2,4},{4,6},{1,3},{3,5},{5,7},{8,10},{10,12},{12,14},{9,11},... | collective-permute-start | bytes 147464 | tf_op jit(solution)/shard_map/ppermute | solution.py:36
  88.7 17.5 %collective-permute-start.31 = (f32[16,6,128]{2,0,1:T(8,128)S(1)}, f32[16,6,128]{2,0,1:T(8,128)S(1)}, u32[]{:S(2)}, u32[]{:S(2)}) collective-permute-start(f32[16,6,128]{2,0,1:T(8,128)S(1)} %get-tuple-element.123), channel_id=1, source_target_pairs={{2,0},{4,2},{6,4},{3,1},{5,3},{7,5},{10,8},{12,10},{14,12},{11,9},... | collective-permute-start | bytes 147464 | tf_op jit(solution)/shard_map/ppermute | solution.py:37
  93.9 6.1 %collective-permute-start.19 = (f32[1,20,128]{2,0,1:T(1,128)S(1)}, f32[1,20,128]{2,0,1:T(1,128)S(1)}, u32[]{:S(2)}, u32[]{:S(2)}) collective-permute-start(f32[1,20,128]{2,0,1:T(1,128)S(1)} %broadcast_select_fusion.24), channel_id=1, source_target_pairs={{0,1},{1,0},{2,3},{3,2},{4,5},{5,4},{6,7},{7,6},{8,9},{9,8},{10,11... | collective-permute-start | bytes 30728 | tf_op jit(solution)/shard_map/ppermute | solution.py:26
  94.1 28.3 %collective-permute-start.17 = (f32[16,6,128]{2,0,1:T(8,128)S(1)}, f32[16,6,128]{2,0,1:T(8,128)S(1)}, u32[]{:S(2)}, u32[]{:S(2)}) collective-permute-start(f32[16,6,128]{2,0,1:T(8,128)S(1)} %get-tuple-element.142), channel_id=1, source_target_pairs={{0,2},{2,4},{4,6},{1,3},{3,5},{5,7},{8,10},{10,12},{12,14},{9,11},... | collective-permute-start | bytes 147464 | tf_op jit(solution)/shard_map/ppermute | solution.py:36
  98.7 23.8 %collective-permute-start.18 = (f32[16,6,128]{2,0,1:T(8,128)S(1)}, f32[16,6,128]{2,0,1:T(8,128)S(1)}, u32[]{:S(2)}, u32[]{:S(2)}) collective-permute-start(f32[16,6,128]{2,0,1:T(8,128)S(1)} %get-tuple-element.143), channel_id=1, source_target_pairs={{2,0},{4,2},{6,4},{3,1},{5,3},{7,5},{10,8},{12,10},{14,12},{11,9},... | collective-permute-start | bytes 147464 | tf_op jit(solution)/shard_map/ppermute | solution.py:37
  101.6 8.5 %collective-permute-start.22 = (f32[16,4,64]{2,0,1:T(8,128)S(1)}, f32[16,4,64]{2,0,1:T(8,128)S(1)}, u32[]{:S(2)}, u32[]{:S(2)}) collective-permute-start(f32[16,4,64]{2,0,1:T(8,128)S(1)} %fusion.5), channel_id=1, source_target_pairs={{0,2},{2,4},{4,6},{6,0},{1,3},{3,5},{5,7},{7,1},{8,10},{10,12},{12... | collective-permute-start | bytes 49160 | tf_op jit(solution)/shard_map/ppermute | solution.py:45
  104.6 5.5 %collective-permute-start.21 = (f32[16,4,64]{2,0,1:T(8,128)S(1)}, f32[16,4,64]{2,0,1:T(8,128)S(1)}, u32[]{:S(2)}, u32[]{:S(2)}) collective-permute-start(f32[16,4,64]{2,0,1:T(8,128)S(1)} %fusion.5), channel_id=1, source_target_pairs={{0,4},{2,6},{4,0},{6,2},{1,5},{3,7},{5,1},{7,3},{8,12},{10,14},{12... | collective-permute-start | bytes 49160 | tf_op jit(solution)/shard_map/ppermute | solution.py:45
  106.2 3.9 %collective-permute-start.20 = (f32[16,4,64]{2,0,1:T(8,128)S(1)}, f32[16,4,64]{2,0,1:T(8,128)S(1)}, u32[]{:S(2)}, u32[]{:S(2)}) collective-permute-start(f32[16,4,64]{2,0,1:T(8,128)S(1)} %fusion.5), channel_id=1, source_target_pairs={{0,6},{2,0},{4,2},{6,4},{1,7},{3,1},{5,3},{7,5},{8,14},{10,8},{12,... | collective-permute-start | bytes 49160 | tf_op jit(solution)/shard_map/ppermute | solution.py:45
  132.3 1.3 collective-permute-start.37
  (22 other events, 177.9 us)
